TPU v7x, 256 devices: a whole 4x4x8 slice. The times are simulated.
256 devices in a mesh: dp: 16 (over z_hi, y, core), tensor: 16 (over z_lo, x).
Axes of the slice: x: 4, y: 4, z: 8 (z_hi: 2, z_lo: 4; z = z_hi * 4 + z_lo), core: 2. Of those that a mesh axis runs over, the one named last changes fastest.
Arguments:
- inputs: bfloat16 [4096, 8192], P('dp', 'tensor'), may hold values from -6 to 6
- gate_pre: bfloat16 [4096, 28672], P('dp', 'tensor'), may hold values from -6 to 6
- up_out: bfloat16 [4096, 28672], P('dp', 'tensor'), may hold values from -6 to 6
- down_weight: bfloat16 [28672, 8192], P('tensor', 'dp'), may hold values from -0.0625 to 0.0625
- out_grad: bfloat16 [4096, 8192], P('dp'), may hold values from -6 to 6
- seed_in: int32 [8192, 64], P('tensor'), may hold values from -2 to 2
- seed_out: int32 [28672, 64], P('tensor'), may hold values from -2 to 2
- queries: bfloat16 [65536, 4096], P(('dp', 'tensor')), may hold values from -0.09375 to 0.09375
Outputs:
- grads: float32 [16, 4096], P('dp')
- scores: float32 [16, 65536], P(None, ('dp', 'tensor'))
All inputs are finite; a program needn't handle non-finite values.
Results may differ from a plain program's by a relative error of at most 0.01.
Values may be sent and summed in bfloat16 or wider, within the bound.
No kernel may reach another device: no remote copies, remote signals or barrier semaphores. Data moves between devices by JAX's collectives and lax.ppermute only.
A program may use at most 128 MiB of HBM per device.

v0:
```python
import jax
import jax.numpy as jnp
from jax import lax
from jax.experimental import pallas as pl
from jax.experimental.pallas import tpu as pltpu
from jax.sharding import Mesh, PartitionSpec as P


D = 8192
FF = 28672
BF = jnp.bfloat16
F32 = jnp.float32
DP = ("zh", "y", "c")
TP = ("zl", "x")
WIDE = 896


def flip(v, axis):
    return lax.ppermute(v, axis, [(0, 1), (1, 0)])


def fetch(v, axis, step):
    return lax.ppermute(v, axis, [((i + step) % 4, i) for i in range(4)])


def everyone(v, axes, count):
    copies = jnp.broadcast_to(v[None], (count,) + v.shape)
    return lax.all_to_all(copies, axes, 0, 0, tiled=True)


def nt(rows, weight):
    return lax.dot_general(rows, weight, (((1,), (1,)), ((), ())), preferred_element_type=F32)


def spec_of(array, width, at):
    if array.ndim == 3:
        return pl.BlockSpec((None, array.shape[1], width), lambda i, s: (s[at], 0, s[at + 1]))
    return pl.BlockSpec((array.shape[0], width), lambda i, s: (0, s[at + 1]))


def near_sums(index, at, rows, mats, act, proj):
    n = len(mats)
    seq, ff = act.shape
    block, rank = mats[0].shape[1], proj.shape[1]

    def kernel(_, *refs):
        parts, mat = refs[:n], refs[n : 2 * n]
        act_ref, proj_ref, out = refs[2 * n :]

        @pl.when(pl.program_id(0) == 0)
        def _():
            out[...] = jnp.zeros_like(out)

        hidden = sum(nt(p[...], m[...]) for p, m in zip(parts, mat))
        grad = (hidden * act_ref[...].astype(F32)).astype(BF)
        out[...] += jnp.dot(grad, proj_ref[...], preferred_element_type=F32)

    return pl.pallas_call(
        kernel,
        out_shape=jax.ShapeDtypeStruct((seq, rank), F32),
        grid_spec=pltpu.PrefetchScalarGridSpec(
            num_scalar_prefetch=1,
            grid=(ff // WIDE,),
            in_specs=[spec_of(rows, block, at + 2 * t) for t in range(n)]
            + [pl.BlockSpec((WIDE, block), lambda i, s: (i, 0))] * n
            + [
                pl.BlockSpec((seq, WIDE), lambda i, s: (0, i)),
                pl.BlockSpec((WIDE, rank), lambda i, s: (i, 0)),
            ],
            out_specs=pl.BlockSpec((seq, rank), lambda i, s: (0, 0)),
        ),
    )(index, *([rows] * n), *mats, act, proj)


def far_sums(index, pieces, mats):
    n = len(mats)
    seq, ff = pieces[0].shape[0], mats[0].shape[0]
    block = mats[0].shape[1]

    def kernel(s, *refs):
        parts, mat = refs[:4], refs[4 : 4 + n]
        out, kept, rows, sems = refs[4 + n :]

        @pl.when(pl.program_id(0) == 0)
        def _():
            copies = [
                pltpu.make_async_copy(parts[r], rows.at[lax.rem(s[1] + r, 4)], sems.at[r])
                for r in range(4)
            ]
            for copy in copies:
                copy.start()
            for copy in copies:
                copy.wait()
            kept[...] = rows[2]

        total = None
        for t in range(n):
            at = pl.multiple_of(s[18 + 2 * t + 1] * block, block)
            term = nt(rows[s[18 + 2 * t], :, pl.ds(at, block)], mat[t][...])
            total = term if total is None else total + term
        out[...] = total

    return pl.pallas_call(
        kernel,
        out_shape=(
            jax.ShapeDtypeStruct((seq, ff), F32),
            jax.ShapeDtypeStruct((seq, 2 * block), BF),
        ),
        grid_spec=pltpu.PrefetchScalarGridSpec(
            num_scalar_prefetch=1,
            grid=(ff // WIDE,),
            in_specs=[pl.BlockSpec(memory_space=pl.ANY)] * 4
            + [pl.BlockSpec((WIDE, block), lambda i, s: (i, 0))] * n,
            out_specs=(
                pl.BlockSpec((seq, WIDE), lambda i, s: (0, i)),
                pl.BlockSpec((seq, 2 * block), lambda i, s: (0, 0)),
            ),
            scratch_shapes=[
                pltpu.VMEM((4, seq, 2 * block), BF),
                pltpu.SemaphoreType.DMA((4,)),
            ],
        ),
    )(index, *pieces, *mats)


def project(index, near_from, far_from, near, far, mats, right, sums, acts, proj, left_all):
    n = len(mats)
    seq, ff = sums.shape
    block, rank = mats[0].shape[1], proj.shape[1]
    half = rank // 2

    def kernel(s, *refs):
        near_parts, far_parts, mat = refs[:n], refs[n : 2 * n], refs[2 * n : 3 * n]
        right_ref, sum_ref, act_n, act_f, proj_ref, left_ref, out, right_n, right_f = refs[3 * n :]

        @pl.when(pl.program_id(0) == 0)
        def _():
            right_n[...] = right_ref[...]
            right_f[...] = jnp.zeros_like(right_f)

        hidden = sum(nt(p[...], m[...]) for p, m in zip(near_parts, mat))
        grad = (hidden * act_n[...].astype(F32)).astype(BF)
        right_n[...] += jnp.dot(grad, proj_ref[...], preferred_element_type=F32)
        hidden = sum_ref[...] + sum(nt(p[...], m[...]) for p, m in zip(far_parts, mat))
        grad = (hidden * act_f[...].astype(F32)).astype(BF)
        right_f[...] += jnp.dot(grad, proj_ref[...], preferred_element_type=F32)

        @pl.when(pl.program_id(0) == pl.num_programs(0) - 1)
        def _():
            zh = s[0]
            pieces = []
            for z, total in ((zh, right_n), (1 - zh, right_f)):
                left = sum(left_ref[4 * z + k].astype(F32) for k in range(4)).astype(BF)
                outer = jnp.dot(left, total[...].astype(BF), preferred_element_type=F32)
                pieces.append(jnp.concatenate([outer[:half], outer[half:]], axis=1).astype(BF))
            for copy in range(out.shape[0]):
                out[copy, :half, :] = pieces[0]
                out[copy, half:, :] = pieces[1]

    wide = pl.BlockSpec((seq, WIDE), lambda i, s: (0, i))
    return_shape = (8, rank, 2 * rank)
    return pl.pallas_call(
        kernel,
        out_shape=jax.ShapeDtypeStruct(return_shape, BF),
        grid_spec=pltpu.PrefetchScalarGridSpec(
            num_scalar_prefetch=1,
            grid=(ff // WIDE,),
            in_specs=[spec_of(near, block, near_from + 2 * t) for t in range(n)]
            + [spec_of(far, block, far_from + 2 * t) for t in range(n)]
            + [pl.BlockSpec((WIDE, block), lambda i, s: (i, 0))] * n
            + [pl.BlockSpec((seq, rank), lambda i, s: (0, 0)), wide, wide, wide]
            + [pl.BlockSpec((WIDE, rank), lambda i, s: (i, 0))]
            + [pl.BlockSpec(left_all.shape, lambda i, s: (0, 0, 0))],
            out_specs=pl.BlockSpec(return_shape, lambda i, s: (0, 0, 0)),
            scratch_shapes=[pltpu.VMEM((seq, rank), F32)] * 2,
        ),
    )(index, *([near] * n), *([far] * n), *mats, right, sums, *acts, proj, left_all)


def merge(parts):
    def kernel(ref, out):
        side = [
            [sum(ref[z, k, g].astype(F32) for k in range(4)) for g in range(2)] for z in range(2)
        ]
        first = (side[0][0] + side[1][1]).astype(BF)
        second = (side[1][0] + side[0][1]).astype(BF)
        for copy in range(out.shape[0]):
            out[copy, 0] = first
            out[copy, 1] = second

    return pl.pallas_call(
        kernel, out_shape=jax.ShapeDtypeStruct((32, 2) + parts.shape[3:], BF)
    )(parts)


def finish(me, parts, queries):
    rows, lanes = parts.shape[-2:]
    count = queries.shape[0]
    examples = parts.shape[0] * parts.shape[2] * parts.shape[3]

    def kernel(me_ref, ref, q_ref, grads_ref, scores_ref, table):
        for y in range(4):
            for core in range(2):
                for z in range(2):
                    e = z * 8 + y * 2 + core
                    table[e * rows : (e + 1) * rows, :] = sum(
                        ref[y, k, core, z].astype(F32) for k in range(4)
                    )
        total = jnp.zeros((examples, count), F32)
        for k in range(rows):
            span = slice(k * lanes, (k + 1) * lanes)
            piece = table[pl.ds(k, examples, stride=rows), :].astype(BF)
            total = total + nt(piece, q_ref[:, span])
            grads_ref[:, span] = table[pl.ds(me_ref[0] * rows + k, 1), :]
        scores_ref[...] = total

    return pl.pallas_call(
        kernel,
        out_shape=(
            jax.ShapeDtypeStruct((1, rows * lanes), F32),
            jax.ShapeDtypeStruct((examples, count), F32),
        ),
        in_specs=[
            pl.BlockSpec(memory_space=pltpu.SMEM),
            pl.BlockSpec(memory_space=pltpu.VMEM),
            pl.BlockSpec(memory_space=pltpu.VMEM),
        ],
        out_specs=(pl.BlockSpec(memory_space=pltpu.VMEM), pl.BlockSpec(memory_space=pltpu.VMEM)),
        scratch_shapes=[pltpu.VMEM((examples * rows, lanes), F32)],
    )(me, parts, queries)


def along_y(v, forward):
    pairs = []
    for y in range(4):
        for core in range(2):
            step = 1 if (core == 0) == forward else 3
            pairs.append((2 * y + core, 2 * ((y + step) % 4) + core))
    return lax.ppermute(v, ("y", "c"), pairs)


def trade(copies, axes):
    return lax.all_to_all(copies, axes, 0, 0, tiled=True)


def on_device(inputs, gate_pre, up_out, weight, out_grad, seed_in, seed_out, queries):
    seq, block = out_grad.shape[0], weight.shape[1]
    rank = seed_in.shape[1]
    zh, y, c, x = (lax.axis_index(name).astype(jnp.int32) for name in ("zh", "y", "c", "x"))

    w_one = along_y(weight, True)
    w_two = along_y(weight, False)
    m_own = flip(weight, "c")
    start = ((1 - zh) * 8 + ((y + x) % 4) * 2) * block
    far = flip(lax.dynamic_slice(out_grad, (0, start), (seq, 2 * block)), "zh")

    proj = (seed_out.astype(F32) * 0.25 * (2.0 * FF) ** (-0.5)).astype(BF)
    gate = gate_pre.astype(F32)
    sigma = jax.nn.sigmoid(gate)
    act = (up_out.astype(F32) * sigma * (1.0 + gate * (1.0 - sigma))).astype(BF)
    one, two = jnp.where(c == 0, 3, 1), jnp.where(c == 0, 1, 3)
    slabs = [(0, c), (0, 1 - c), (one, c), (two, 1 - c), (two, c), (one, 1 - c), (2, c), (2, 1 - c)]
    index = [zh, x]
    for j, core in slabs:
        index += [zh, zh * 8 + ((y + j) % 4) * 2 + core]
    for j, core in slabs:
        index += [jnp.int32(j), core]
    index = jnp.stack([jnp.asarray(v, jnp.int32) for v in index])
    act, proj, index = lax.optimization_barrier((act, proj, index))
    act_far = flip(act, "zh")

    order = jnp.concatenate([jnp.arange(0, rank, 2), jnp.arange(1, rank, 2)])
    pick = (jnp.arange(rank)[:, None] == order[None, :]).astype(BF)
    proj_in = (seed_in.astype(F32) * (2.0 * D) ** (-0.5)).astype(BF)
    proj_in = jnp.dot(proj_in, pick, preferred_element_type=F32).astype(BF)
    left = lax.dot_general(
        proj_in, inputs, (((0,), (1,)), ((), ())), preferred_element_type=F32
    ).astype(BF)
    left = sum(fetch(left, "x", s).astype(F32) for s in (1, 2, 3)) + left.astype(F32)
    left_all = everyone(left.astype(BF), ("zh", "zl"), 8)

    fars = [far] + [fetch(far, "x", s) for s in (1, 2, 3)]

    m_one = flip(w_one, "c")
    m_two = flip(w_two, "c")
    w_opp = along_y(w_one, True)
    m_opp = flip(w_opp, "c")

    mats = (weight, m_own, w_one, m_one, w_two, m_two)
    right = near_sums(index, 2, out_grad, mats, act, proj)
    sum_far, far_opp = far_sums(index, fars, mats)
    payload = project(
        index, 14, 30, out_grad, far_opp, (w_opp, m_opp), right, sum_far, (act, act_far), proj,
        left_all,
    )
    z_all = trade(payload, ("zh", "zl"))
    merged = merge(z_all.reshape(2, 4, 2, rank // 2, 2 * rank))
    every = trade(merged, ("y", "x", "c"))
    me = (zh * 8 + y * 2 + c).reshape(1)
    every = every.reshape(4, 4, 2, 2, rank // 2, 2 * rank)
    return finish(me, every, queries)


def solution(mesh):
    fine = Mesh(mesh.devices.reshape(2, 4, 2, 4, 4), DP + TP)
    in_specs = (
        P(DP, TP),
        P(DP, TP),
        P(DP, TP),
        P(TP, DP),
        P(DP, None),
        P(TP, None),
        P(TP, None),
        P(DP + TP, None),
    )
    out_specs = (P(DP, None), P(None, DP + TP))

    return jax.shard_map(
        on_device, mesh=fine, in_specs=in_specs, out_specs=out_specs, check_vma=False
    )
```

profile of v0, /device:TPU:1, one launch (start us, length us, event | category | flops | bytes accessed | tf_op | source)
XLA Modules:
  0.0 200.7 jit_solution(5148052743798398052)
XLA Ops:
  0.6 3.6 %collective-permute-start.5 = (bf16[1792,512]{1,0:T(8,128)(2,1)}, bf16[1792,512]{1,0:T(8,128)(2,1)S(1)}, u32[]{:S(2)}, u32[]{:S(2)}) collective-permute-start(bf16[1792,512]{1,0:T(8,128)(2,1)} %refs_6_.1), channel_id=1, source_target_pairs={{0,32},{16,112},{32,64},{48,16},{64,96},{80,48},{96,0},{112,80},{1... | collective-permute-start | bytes 5505032 | tf_op jit(solution)/shard_map/ppermute | solution.py:239
  4.3 37.1 %collective-permute-done.5.refs_6_.refs_8_ = bf16[1792,512]{1,0:T(8,128)(2,1)S(1)} collective-permute-done((bf16[1792,512]{1,0:T(8,128)(2,1)}, bf16[1792,512]{1,0:T(8,128)(2,1)S(1)}, u32[]{:S(2)}, u32[]{:S(2)}) %collective-permute-start.5) | collective-permute-done | bytes 1835040 | tf_op jit(solution)/shard_map/ppermute | solution.py:239
  41.4 3.4 %collective-permute-start.9 = (bf16[1792,512]{1,0:T(8,128)(2,1)S(1)}, bf16[1792,512]{1,0:T(8,128)(2,1)}, u32[]{:S(2)}, u32[]{:S(2)}) collective-permute-start(bf16[1792,512]{1,0:T(8,128)(2,1)S(1)} %collective-permute-done.5.refs_6_.refs_8_), channel_id=1, source_target_pairs={{0,32},{16,112},{32,64},{48,16},{64,96},{80,48},{96,0},{112,80},{1... | collective-permute-start | bytes 5505032 | tf_op jit(solution)/shard_map/ppermute | solution.py:239
  44.8 3.4 %collective-permute-start.4 = (bf16[1792,512]{1,0:T(8,128)(2,1)}, bf16[1792,512]{1,0:T(8,128)(2,1)}, u32[]{:S(2)}, u32[]{:S(2)}) collective-permute-start(bf16[1792,512]{1,0:T(8,128)(2,1)} %refs_6_.1), channel_id=1, source_target_pairs={{0,16},{16,0},{1,17},{17,1},{2,18},{18,2},{3,19},{19,3},{4,20},{20... | collective-permute-start | bytes 5505032 | tf_op jit(solution)/shard_map/ppermute | solution.py:19
  48.7 1.3 fusion.7
  50.1 1.0 collective-permute-start.12
  51.1 1.3 copy.10
  52.4 0.9 collective-permute-done.12
  53.3 1.2 collective-permute-start.13
  54.5 10.5 %collective-permute-done.9.refs_4_ = bf16[1792,512]{1,0:T(8,128)(2,1)} collective-permute-done((bf16[1792,512]{1,0:T(8,128)(2,1)S(1)}, bf16[1792,512]{1,0:T(8,128)(2,1)}, u32[]{:S(2)}, u32[]{:S(2)}) %collective-permute-start.9) | collective-permute-done | bytes 1835040 | tf_op jit(solution)/shard_map/ppermute | solution.py:239
  64.9 7.7 %collective-permute-start.10 = (bf16[1792,512]{1,0:T(8,128)(2,1)}, bf16[1792,512]{1,0:T(8,128)(2,1)}, u32[]{:S(2)}, u32[]{:S(2)}) collective-permute-start(bf16[1792,512]{1,0:T(8,128)(2,1)} %collective-permute-done.9.refs_4_), channel_id=1, source_target_pairs={{0,16},{16,0},{1,17},{17,1},{2,18},{18,2},{3,19},{19,3},{4,20},{20... | collective-permute-start | bytes 5505032 | tf_op jit(solution)/shard_map/ppermute | solution.py:19
  72.7 0.9 multiply_convert_fusion.refs_13_.refs_10_
  73.6 1.9 constant_dynamic-slice_fusion
  76.2 1.4 collective-permute-done.14
  78.2 3.7 %collective-permute-start = (bf16[256,1024]{1,0:T(8,128)(2,1)}, bf16[256,1024]{1,0:T(8,128)(2,1)S(1)}, u32[]{:S(2)}, u32[]{:S(2)}) collective-permute-start(bf16[256,1024]{1,0:T(8,128)(2,1)} %constant_dynamic-slice_fusion), channel_id=1, source_target_pairs={{0,128},{128,0},{1,129},{129,1},{2,130},{130,2},{3,131},{131,3},{4... | collective-permute-start | bytes 1572872 | tf_op jit(solution)/shard_map/ppermute | solution.py:19
  81.9 2.2 %fusion.5.refs_12_.refs_8_ = bf16[256,1792]{1,0:T(8,128)(2,1)S(1)} fusion(bf16[256,1792]{1,0:T(8,128)(2,1)} %param.9, bf16[256,1792]{1,0:T(8,128)(2,1)} %param.10), kind=kLoop, calls=%fused_computation.7 | loop fusion | flops 5046272 | bytes 2752512 | tf_op jit(solution)/shard_map/convert_element_type | solution.py:260
  84.1 18.7 %collective-permute-done.refs_0_ = bf16[256,1024]{1,0:T(8,128)(2,1)S(1)} collective-permute-done((bf16[256,1024]{1,0:T(8,128)(2,1)}, bf16[256,1024]{1,0:T(8,128)(2,1)S(1)}, u32[]{:S(2)}, u32[]{:S(2)}) %collective-permute-start) | collective-permute-done | bytes 524320 | tf_op jit(solution)/shard_map/ppermute | solution.py:19
  102.8 7.4 %collective-permute-start.11 = (bf16[256,1792]{1,0:T(8,128)(2,1)S(1)}, bf16[256,1792]{1,0:T(8,128)(2,1)}, u32[]{:S(2)}, u32[]{:S(2)}) collective-permute-start(bf16[256,1792]{1,0:T(8,128)(2,1)S(1)} %fusion.5.refs_12_.refs_8_), channel_id=1, source_target_pairs={{0,128},{128,0},{1,129},{129,1},{2,130},{130,2},{3,131},{131,3},{4... | collective-permute-start | bytes 2752520 | tf_op jit(solution)/shard_map/ppermute | solution.py:19
  110.2 1.3 collective-permute-start.1
  113.0 3.6 %all-to-all-start = ((bf16[8,64,256]{2,1,0:T(8,128)(2,1)}), bf16[8,64,256]{2,1,0:T(8,128)(2,1)S(1)}, u32[]{:S(2)}, u32[]{:S(2)}) async-start(bf16[8,64,256]{2,1,0:T(8,128)(2,1)} %broadcast_in_dim.2), calls=%async_computation | async-start | bytes 524288 | tf_op jit(solution)/shard_map/all_to_all | solution.py:28
  116.7 9.3 %shard_map.96.refs_6_ = f32[256,64]{1,0:T(8,128)} custom-call(s32[34]{0:T(128)} %stack.75.s._, bf16[256,8192]{1,0:T(8,128)(2,1)} %refs_1_.3, bf16[256,8192]{1,0:T(8,128)(2,1)} %refs_1_.3, bf16[256,8192]{1,0:T(8,128)(2,1)} %refs_1_.3, bf16[256,8192]{1,0:T(8,128)(2,1)} %refs_1_.3, bf16[256,8192]{1,0:T(8,128)(2,1)} %refs_1_.3, bf16[256,8192]{1,0:T(8,128)(2,1)} %refs_1_.3, ...), custom_call_target="tpu_custom_call" | custom-call | tf_op jit(solution)/shard_map/pallas_call | solution.py:58
  126.0 11.8 %collective-permute-done.3.refs_3_ = bf16[256,1024]{1,0:T(8,128)(2,1)S(1)} collective-permute-done((bf16[256,1024]{1,0:T(8,128)(2,1)S(1)}, bf16[256,1024]{1,0:T(8,128)(2,1)S(1)}, u32[]{:S(2)}, u32[]{:S(2)}) %collective-permute-start.3) | collective-permute-done | bytes 524320 | tf_op jit(solution)/shard_map/ppermute | solution.py:23
  137.9 0.8 copy-done.7
  138.7 10.3 %shard_map.95 = (f32[256,1792]{1,0:T(8,128)}, bf16[256,1024]{1,0:T(8,128)(2,1)}) custom-call(s32[34]{0:T(128)} %stack.75.s._, bf16[256,1024]{1,0:T(8,128)(2,1)} %copy-done.5, bf16[256,1024]{1,0:T(8,128)(2,1)} %collective-permute-done.1.refs_1_, bf16[256,1024]{1,0:T(8,128)(2,1)} %copy-done.6, bf16[256,1024]{1,0:T(8,128)(2,1)} %copy-done.7, ...), custom_call_target="tpu_custom_call" | custom-call | tf_op jit(solution)/shard_map/pallas_call | solution.py:103
  149.0 6.2 %all-to-all-done.refs_11_ = bf16[8,64,256]{2,1,0:T(8,128)(2,1)S(1)} async-done(((bf16[8,64,256]{2,1,0:T(8,128)(2,1)}), bf16[8,64,256]{2,1,0:T(8,128)(2,1)S(1)}, u32[]{:S(2)}, u32[]{:S(2)}) %all-to-all-start) | async-done | bytes 262176 | tf_op jit(solution)/shard_map/all_to_all | solution.py:28
  155.9 7.7 %shard_map.97 = bf16[8,64,128]{2,1,0:T(8,128)(2,1)} custom-call(s32[34]{0:T(128)} %stack.75.s._, bf16[256,8192]{1,0:T(8,128)(2,1)} %refs_1_.3, bf16[256,8192]{1,0:T(8,128)(2,1)} %refs_1_.3, bf16[256,1024]{1,0:T(8,128)(2,1)} %get-tuple-element.8.refs_2_.refs_3_, bf16[256,1024]{1,0:T(8,128)(2,1)} %get-tuple-element.8.refs_2_.refs_3_, ...), custom_call_target="tpu_custom_call" | custom-call | tf_op jit(solution)/shard_map/pallas_call | solution.py:162
  163.6 12.3 %all_to_all.15 = bf16[8,64,128]{2,1,0:T(8,128)(2,1)} all-to-all(bf16[8,64,128]{2,1,0:T(8,128)(2,1)} %shard_map.97), channel_id=1, replica_groups=mesh['zh'=2,'y'=4,'c'=2,'zl'=4,'x'=4] {'zh','zl'}, dimensions={0} | all-to-all | bytes 262144 | tf_op jit(solution)/shard_map/all_to_all | solution.py:243
  175.8 1.8 shard_map.98
  177.6 7.8 %all-to-all-start.2 = ((bf16[32,2,32,128]{3,2,1,0:T(8,128)(2,1)}), bf16[32,2,32,128]{3,2,1,0:T(8,128)(2,1)S(1)}, u32[]{:S(2)}, u32[]{:S(2)}) async-start(bf16[32,2,32,128]{3,2,1,0:T(8,128)(2,1)} %shard_map.98), calls=%async_computation.2 | async-start | bytes 1048576 | tf_op jit(solution)/shard_map/all_to_all | solution.py:243
  185.4 11.4 %all-to-all-done.2 = bf16[32,2,32,128]{3,2,1,0:T(8,128)(2,1)S(1)} async-done(((bf16[32,2,32,128]{3,2,1,0:T(8,128)(2,1)}), bf16[32,2,32,128]{3,2,1,0:T(8,128)(2,1)S(1)}, u32[]{:S(2)}, u32[]{:S(2)}) %all-to-all-start.2) | async-done | bytes 524320 | tf_op jit(solution)/shard_map/all_to_all | solution.py:243
  196.8 0.8 copy-done.3
  197.6 3.1 %shard_map.99 = (f32[1,4096]{1,0:T(1,128)}, f32[16,256]{1,0:T(8,128)}) custom-call(s32[1]{0:T(128)} %bitcast.me_ref, bf16[4,4,2,2,32,128]{5,4,3,2,1,0:T(8,128)(2,1)} %bitcast.18, bf16[256,4096]{1,0:T(8,128)(2,1)} %q_ref.1), custom_call_target="tpu_custom_call" | custom-call | tf_op jit(solution)/shard_map/pallas_call | solution.py:217
  (50 shorter events, 4.1 us)
Async XLA Ops:
  0.6 48.1 %copy-start = (bf16[256,512]{1,0:T(8,128)(2,1)S(1)}, bf16[256,512]{1,0:T(8,128)(2,1)}, u32[]{:S(2)}) copy-start(bf16[256,512]{1,0:T(8,128)(2,1)} %param.8) | copy-start | bytes 786436
  0.6 40.7 %collective-permute-start.5 = (bf16[1792,512]{1,0:T(8,128)(2,1)}, bf16[1792,512]{1,0:T(8,128)(2,1)S(1)}, u32[]{:S(2)}, u32[]{:S(2)}) collective-permute-start(bf16[1792,512]{1,0:T(8,128)(2,1)} %refs_6_.1), channel_id=1, source_target_pairs={{0,32},{16,112},{32,64},{48,16},{64,96},{80,48},{96,0},{112,80},{1... | collective-permute-start | bytes 5505032 | tf_op jit(solution)/shard_map/ppermute | solution.py:239
  4.3 44.0 %collective-permute-start.7 = (bf16[1792,512]{1,0:T(8,128)(2,1)}, bf16[1792,512]{1,0:T(8,128)(2,1)}, u32[]{:S(2)}, u32[]{:S(2)}) collective-permute-start(bf16[1792,512]{1,0:T(8,128)(2,1)} %refs_6_.1), channel_id=1, source_target_pairs={{0,96},{16,48},{32,0},{48,80},{64,32},{80,112},{96,64},{112,16},{1... | collective-permute-start | bytes 5505032 | tf_op jit(solution)/shard_map/ppermute | solution.py:239
  41.4 34.1 %copy-start.2 = (bf16[1792,512]{1,0:T(8,128)(2,1)}, bf16[1792,512]{1,0:T(8,128)(2,1)S(1)}, u32[]{:S(2)}) copy-start(bf16[1792,512]{1,0:T(8,128)(2,1)S(1)} %collective-permute-done.5.refs_6_.refs_8_) | copy-start | bytes 5505028
  41.4 23.6 %collective-permute-start.9 = (bf16[1792,512]{1,0:T(8,128)(2,1)S(1)}, bf16[1792,512]{1,0:T(8,128)(2,1)}, u32[]{:S(2)}, u32[]{:S(2)}) collective-permute-start(bf16[1792,512]{1,0:T(8,128)(2,1)S(1)} %collective-permute-done.5.refs_6_.refs_8_), channel_id=1, source_target_pairs={{0,32},{16,112},{32,64},{48,16},{64,96},{80,48},{96,0},{112,80},{1... | collective-permute-start | bytes 5505032 | tf_op jit(solution)/shard_map/ppermute | solution.py:239
  44.8 65.5 %collective-permute-start.4 = (bf16[1792,512]{1,0:T(8,128)(2,1)}, bf16[1792,512]{1,0:T(8,128)(2,1)}, u32[]{:S(2)}, u32[]{:S(2)}) collective-permute-start(bf16[1792,512]{1,0:T(8,128)(2,1)} %refs_6_.1), channel_id=1, source_target_pairs={{0,16},{16,0},{1,17},{17,1},{2,18},{18,2},{3,19},{19,3},{4,20},{20... | collective-permute-start | bytes 5505032 | tf_op jit(solution)/shard_map/ppermute | solution.py:19
  48.1 63.5 %collective-permute-start.6 = (bf16[1792,512]{1,0:T(8,128)(2,1)S(1)}, bf16[1792,512]{1,0:T(8,128)(2,1)}, u32[]{:S(2)}, u32[]{:S(2)}) collective-permute-start(bf16[1792,512]{1,0:T(8,128)(2,1)S(1)} %collective-permute-done.5.refs_6_.refs_8_), channel_id=1, source_target_pairs={{0,16},{16,0},{1,17},{17,1},{2,18},{18,2},{3,19},{19,3},{4,20},{20... | collective-permute-start | bytes 5505032 | tf_op jit(solution)/shard_map/ppermute | solution.py:19
  48.2 63.4 %collective-permute-start.8 = (bf16[1792,512]{1,0:T(8,128)(2,1)}, bf16[1792,512]{1,0:T(8,128)(2,1)}, u32[]{:S(2)}, u32[]{:S(2)}) collective-permute-start(bf16[1792,512]{1,0:T(8,128)(2,1)} %collective-permute-done.7.refs_8_.refs_10_), channel_id=1, source_target_pairs={{0,16},{16,0},{1,17},{17,1},{2,18},{18,2},{3,19},{19,3},{4,20},{20... | collective-permute-start | bytes 5505032 | tf_op jit(solution)/shard_map/ppermute | solution.py:19
  50.1 25.4 %copy-start.8 = (bf16[64,256]{1,0:T(8,128)(2,1)}, bf16[64,256]{1,0:T(8,128)(2,1)S(1)}, u32[]{:S(2)}) copy-start(bf16[64,256]{1,0:T(8,128)(2,1)S(1)} %fusion.7) | copy-start | bytes 98308
  50.1 3.2 %collective-permute-start.12 = (bf16[64,256]{1,0:T(8,128)(2,1)S(1)}, bf16[64,256]{1,0:T(8,128)(2,1)S(1)}, u32[]{:S(2)}, u32[]{:S(2)}) collective-permute-start(bf16[64,256]{1,0:T(8,128)(2,1)S(1)} %fusion.7), channel_id=1, source_target_pairs={{1,0},{2,1},{3,2},{0,3},{5,4},{6,5},{7,6},{4,7},{9,8},{10,9},{11,1... | collective-permute-start | bytes 98312 | tf_op jit(solution)/shard_map/ppermute | solution.py:23
  53.3 22.9 %copy-start.10 = (bf16[64,256]{1,0:T(8,128)(2,1)}, bf16[64,256]{1,0:T(8,128)(2,1)S(1)}, u32[]{:S(2)}) copy-start(bf16[64,256]{1,0:T(8,128)(2,1)S(1)} %collective-permute-done.12) | copy-start | bytes 98308
  53.3 20.2 %collective-permute-start.13 = (bf16[64,256]{1,0:T(8,128)(2,1)S(1)}, bf16[64,256]{1,0:T(8,128)(2,1)S(1)}, u32[]{:S(2)}, u32[]{:S(2)}) collective-permute-start(bf16[64,256]{1,0:T(8,128)(2,1)S(1)} %fusion.7), channel_id=1, source_target_pairs={{2,0},{3,1},{0,2},{1,3},{6,4},{7,5},{4,6},{5,7},{10,8},{11,9},{8,1... | collective-permute-start | bytes 98312 | tf_op jit(solution)/shard_map/ppermute | solution.py:23
  64.9 90.2 %collective-permute-start.10 = (bf16[1792,512]{1,0:T(8,128)(2,1)}, bf16[1792,512]{1,0:T(8,128)(2,1)}, u32[]{:S(2)}, u32[]{:S(2)}) collective-permute-start(bf16[1792,512]{1,0:T(8,128)(2,1)} %collective-permute-done.9.refs_4_), channel_id=1, source_target_pairs={{0,16},{16,0},{1,17},{17,1},{2,18},{18,2},{3,19},{19,3},{4,20},{20... | collective-permute-start | bytes 5505032 | tf_op jit(solution)/shard_map/ppermute | solution.py:19
  73.6 2.6 %copy-start.12 = (bf16[64,256]{1,0:T(8,128)(2,1)}, bf16[64,256]{1,0:T(8,128)(2,1)S(1)}, u32[]{:S(2)}) copy-start(bf16[64,256]{1,0:T(8,128)(2,1)S(1)} %collective-permute-done.13) | copy-start | bytes 98308
  73.6 4.0 %collective-permute-start.14 = (bf16[64,256]{1,0:T(8,128)(2,1)S(1)}, bf16[64,256]{1,0:T(8,128)(2,1)S(1)}, u32[]{:S(2)}, u32[]{:S(2)}) collective-permute-start(bf16[64,256]{1,0:T(8,128)(2,1)S(1)} %fusion.7), channel_id=1, source_target_pairs={{3,0},{0,1},{1,2},{2,3},{7,4},{4,5},{5,6},{6,7},{11,8},{8,9},{9,10... | collective-permute-start | bytes 98312 | tf_op jit(solution)/shard_map/ppermute | solution.py:23
  76.2 36.1 %copy-start.9 = (bf16[64,256]{1,0:T(8,128)(2,1)S(1)}, bf16[64,256]{1,0:T(8,128)(2,1)}, u32[]{:S(2)}) copy-start(bf16[64,256]{1,0:T(8,128)(2,1)} %copy-done.8) | copy-start | bytes 98308
  78.1 34.1 %copy-start.11 = (bf16[64,256]{1,0:T(8,128)(2,1)S(1)}, bf16[64,256]{1,0:T(8,128)(2,1)}, u32[]{:S(2)}) copy-start(bf16[64,256]{1,0:T(8,128)(2,1)} %copy-done.10) | copy-start | bytes 98308
  78.1 34.1 %copy-start.13 = (bf16[64,256]{1,0:T(8,128)(2,1)S(1)}, bf16[64,256]{1,0:T(8,128)(2,1)}, u32[]{:S(2)}) copy-start(bf16[64,256]{1,0:T(8,128)(2,1)} %copy-done.12) | copy-start | bytes 98308
  78.2 24.7 %collective-permute-start = (bf16[256,1024]{1,0:T(8,128)(2,1)}, bf16[256,1024]{1,0:T(8,128)(2,1)S(1)}, u32[]{:S(2)}, u32[]{:S(2)}) collective-permute-start(bf16[256,1024]{1,0:T(8,128)(2,1)} %constant_dynamic-slice_fusion), channel_id=1, source_target_pairs={{0,128},{128,0},{1,129},{129,1},{2,130},{130,2},{3,131},{131,3},{4... | collective-permute-start | bytes 1572872 | tf_op jit(solution)/shard_map/ppermute | solution.py:19
  81.9 30.4 %copy-start.15 = (bf16[64,256]{1,0:T(8,128)(2,1)S(1)}, bf16[64,256]{1,0:T(8,128)(2,1)}, u32[]{:S(2)}) copy-start(bf16[64,256]{1,0:T(8,128)(2,1)} %copy-done.14) | copy-start | bytes 98308
  84.1 32.6 %copy-start.1 = (bf16[256,1792]{1,0:T(8,128)(2,1)}, bf16[256,1792]{1,0:T(8,128)(2,1)S(1)}, u32[]{:S(2)}) copy-start(bf16[256,1792]{1,0:T(8,128)(2,1)S(1)} %fusion.5.refs_12_.refs_8_) | copy-start | bytes 2752516
  102.8 23.2 %copy-start.5 = (bf16[256,1024]{1,0:T(8,128)(2,1)}, bf16[256,1024]{1,0:T(8,128)(2,1)S(1)}, u32[]{:S(2)}) copy-start(bf16[256,1024]{1,0:T(8,128)(2,1)S(1)} %collective-permute-done.refs_0_) | copy-start | bytes 1572868
  102.8 52.3 %collective-permute-start.11 = (bf16[256,1792]{1,0:T(8,128)(2,1)S(1)}, bf16[256,1792]{1,0:T(8,128)(2,1)}, u32[]{:S(2)}, u32[]{:S(2)}) collective-permute-start(bf16[256,1792]{1,0:T(8,128)(2,1)S(1)} %fusion.5.refs_12_.refs_8_), channel_id=1, source_target_pairs={{0,128},{128,0},{1,129},{129,1},{2,130},{130,2},{3,131},{131,3},{4... | collective-permute-start | bytes 2752520 | tf_op jit(solution)/shard_map/ppermute | solution.py:19
  110.2 15.8 %collective-permute-start.1 = (bf16[256,1024]{1,0:T(8,128)(2,1)S(1)}, bf16[256,1024]{1,0:T(8,128)(2,1)}, u32[]{:S(2)}, u32[]{:S(2)}) collective-permute-start(bf16[256,1024]{1,0:T(8,128)(2,1)S(1)} %collective-permute-done.refs_0_), channel_id=1, source_target_pairs={{1,0},{2,1},{3,2},{0,3},{5,4},{6,5},{7,6},{4,7},{9,8},{10,9},{11,1... | collective-permute-start | bytes 1572872 | tf_op jit(solution)/shard_map/ppermute | solution.py:23
  111.6 14.4 %collective-permute-start.2 = (bf16[256,1024]{1,0:T(8,128)(2,1)S(1)}, bf16[256,1024]{1,0:T(8,128)(2,1)S(1)}, u32[]{:S(2)}, u32[]{:S(2)}) collective-permute-start(bf16[256,1024]{1,0:T(8,128)(2,1)S(1)} %collective-permute-done.refs_0_), channel_id=1, source_target_pairs={{2,0},{3,1},{0,2},{1,3},{6,4},{7,5},{4,6},{5,7},{10,8},{11,9},{8,1... | collective-permute-start | bytes 1572872 | tf_op jit(solution)/shard_map/ppermute | solution.py:23
  111.6 26.3 %collective-permute-start.3 = (bf16[256,1024]{1,0:T(8,128)(2,1)S(1)}, bf16[256,1024]{1,0:T(8,128)(2,1)S(1)}, u32[]{:S(2)}, u32[]{:S(2)}) collective-permute-start(bf16[256,1024]{1,0:T(8,128)(2,1)S(1)} %collective-permute-done.refs_0_), channel_id=1, source_target_pairs={{3,0},{0,1},{1,2},{2,3},{7,4},{4,5},{5,6},{6,7},{11,8},{8,9},{9,10... | collective-permute-start | bytes 1572872 | tf_op jit(solution)/shard_map/ppermute | solution.py:23
  113.0 42.1 %all-to-all-start = ((bf16[8,64,256]{2,1,0:T(8,128)(2,1)}), bf16[8,64,256]{2,1,0:T(8,128)(2,1)S(1)}, u32[]{:S(2)}, u32[]{:S(2)}) async-start(bf16[8,64,256]{2,1,0:T(8,128)(2,1)} %broadcast_in_dim.2), calls=%async_computation | async-start | bytes 524288 | tf_op jit(solution)/shard_map/all_to_all | solution.py:28
  126.0 11.8 %copy-start.6 = (bf16[256,1024]{1,0:T(8,128)(2,1)}, bf16[256,1024]{1,0:T(8,128)(2,1)S(1)}, u32[]{:S(2)}) copy-start(bf16[256,1024]{1,0:T(8,128)(2,1)S(1)} %collective-permute-done.2.refs_2_) | copy-start | bytes 1572868
  137.9 0.8 copy-start.7
  155.2 0.7 copy-start.4
  177.6 19.2 %all-to-all-start.2 = ((bf16[32,2,32,128]{3,2,1,0:T(8,128)(2,1)}), bf16[32,2,32,128]{3,2,1,0:T(8,128)(2,1)S(1)}, u32[]{:S(2)}, u32[]{:S(2)}) async-start(bf16[32,2,32,128]{3,2,1,0:T(8,128)(2,1)} %shard_map.98), calls=%async_computation.2 | async-start | bytes 1048576 | tf_op jit(solution)/shard_map/all_to_all | solution.py:243
  196.8 0.8 copy-start.3
  (1 other events, 0.6 us)
where the time goes:
time: 201 us
  waiting for transfers between devices  98 us (49%)
  starting transfers between devices  45.4 us (23%)
  Pallas kernels  32.1 us (16%)
  blocking collectives  12.3 us (6%)
  local copies, waits for them, and re-layouts  7.58 us (4%)
  other arithmetic  3.21 us (2%)
    ppermute x3, waiting for transfers between devices, along_y(): return lax.ppermute(v, ('y', 'c'), pairs)  47.5 us
    ppermute x6, starting transfers between devices, flip(): return lax.ppermute(v, axis, [(0, 1), (1, 0)])  22.7 us
    ppermute x6, waiting for transfers between devices, flip(): return lax.ppermute(v, axis, [(0, 1), (1, 0)])  18.8 us
    ppermute x6, waiting for transfers between devices, fetch(): return lax.ppermute(v, axis, [((i + step) % 4, i) for i in range(4)])  14.1 us
    all_to_all x1, blocking collectives, trade(): return lax.all_to_all(copies, axes, 0, 0, tiled=True)  12.3 us
    all_to_all x1, waiting for transfers between devices, trade(): return lax.all_to_all(copies, axes, 0, 0, tiled=True)  11.4 us
    pallas_call x1, Pallas kernels, far_sums(): pl.pallas_call(kernel, out_shape=(jax.ShapeDtypeStruct((seq, ff), F32), j...  10.3 us
    pallas_call x1, Pallas kernels, near_sums(): pl.pallas_call(kernel, out_shape=jax.ShapeDtypeStruct((seq, rank), F32),...  9.31 us
  transfers between devices with their start and end apart: 17, of which 8 were waited for; matrix products, arithmetic and copies ran while one was open for 5% of the time, Pallas kernels for 10%

commit v1 on v0

v1 whole, which is shorter than its diff:
```python
import jax
import jax.numpy as jnp
from jax import lax
from jax.experimental import pallas as pl
from jax.experimental.pallas import tpu as pltpu
from jax.sharding import Mesh, PartitionSpec as P


D = 8192
FF = 28672
BF = jnp.bfloat16
F32 = jnp.float32
DP = ("zh", "y", "c")
TP = ("zl", "x")
WIDE = 896
TILE = 256


def flip(v, axis):
    return lax.ppermute(v, axis, [(0, 1), (1, 0)])


def fetch(v, axis, step):
    return lax.ppermute(v, axis, [((i + step) % 4, i) for i in range(4)])


def everyone(v, axes, count):
    copies = jnp.broadcast_to(v[None], (count,) + v.shape)
    return lax.all_to_all(copies, axes, 0, 0, tiled=True)


def nt(rows, weight):
    return lax.dot_general(rows, weight, (((1,), (1,)), ((), ())), preferred_element_type=F32)


def slab_sums(index, near, pieces_a, pieces_b, mats, act, proj):
    n = len(mats)
    seq, ff = act.shape
    block, rank = mats[0].shape[1], proj.shape[1]
    half, pair = seq // 2, 2 * block

    def kernel(s, *refs):
        near_ref, parts_a, parts_b, mat = refs[0], refs[1:5], refs[5:9], refs[9 : 9 + n]
        act_ref, proj_ref, right, out, kept, rows, sems = refs[9 + n :]

        @pl.when(pl.program_id(0) == 0)
        def _():
            copies = []
            for j in range(4):
                at = pl.multiple_of(s[4 + j] * block, block)
                source = near_ref.at[:, pl.ds(at, pair)]
                copies.append((source, rows.at[j, pl.ds(0, seq)]))
            for r in range(4):
                slot = lax.rem(s[1] + r, 4)
                at_a = pl.multiple_of(seq + s[2] * half, half)
                at_b = pl.multiple_of(seq + (1 - s[2]) * half, half)
                copies.append((parts_a[r], rows.at[slot, pl.ds(at_a, half)]))
                copies.append((parts_b[r], rows.at[slot, pl.ds(at_b, half)]))
            copies = [
                pltpu.make_async_copy(source, target, sems.at[k])
                for k, (source, target) in enumerate(copies)
            ]
            for copy in copies:
                copy.start()
            for copy in copies:
                copy.wait()
            kept[...] = rows[2]
            right[...] = jnp.zeros_like(right)

        total = None
        for t in range(n):
            at = pl.multiple_of(s[8 + 2 * t + 1] * block, block)
            term = nt(rows[s[8 + 2 * t], :, pl.ds(at, block)], mat[t][...])
            total = term if total is None else total + term
        out[...] = total[seq:]
        grad = (total[:seq] * act_ref[...].astype(F32)).astype(BF)
        right[...] += jnp.dot(grad, proj_ref[...], preferred_element_type=F32)

    return pl.pallas_call(
        kernel,
        out_shape=(
            jax.ShapeDtypeStruct((seq, rank), F32),
            jax.ShapeDtypeStruct((seq, ff), F32),
            jax.ShapeDtypeStruct((2 * seq, pair), BF),
        ),
        grid_spec=pltpu.PrefetchScalarGridSpec(
            num_scalar_prefetch=1,
            grid=(ff // TILE,),
            in_specs=[pl.BlockSpec(memory_space=pl.ANY)] * 9
            + [pl.BlockSpec((TILE, block), lambda i, s: (i, 0))] * n
            + [
                pl.BlockSpec((seq, TILE), lambda i, s: (0, i)),
                pl.BlockSpec((TILE, rank), lambda i, s: (i, 0)),
            ],
            out_specs=(
                pl.BlockSpec((seq, rank), lambda i, s: (0, 0)),
                pl.BlockSpec((seq, TILE), lambda i, s: (0, i)),
                pl.BlockSpec((2 * seq, pair), lambda i, s: (0, 0)),
            ),
            scratch_shapes=[
                pltpu.VMEM((4, 2 * seq, pair), BF),
                pltpu.SemaphoreType.DMA((12,)),
            ],
        ),
    )(index, near, *pieces_a, *pieces_b, *mats, act, proj)


def middle(index, rows, mat, right, sums, act, proj):
    seq, ff = sums.shape
    block, rank = mat.shape[1], proj.shape[1]

    def kernel(_, rows_ref, mat_ref, right_ref, sum_ref, act_ref, proj_ref, out, sum_out):
        @pl.when(pl.program_id(0) == 0)
        def _():
            out[...] = right_ref[...]

        total = nt(rows_ref[...], mat_ref[...])
        sum_out[...] = sum_ref[...] + total[seq:]
        grad = (total[:seq] * act_ref[...].astype(F32)).astype(BF)
        out[...] += jnp.dot(grad, proj_ref[...], preferred_element_type=F32)

    wide = pl.BlockSpec((seq, WIDE), lambda i, s: (0, i))
    small = pl.BlockSpec((seq, rank), lambda i, s: (0, 0))
    return pl.pallas_call(
        kernel,
        out_shape=(jax.ShapeDtypeStruct((seq, rank), F32), jax.ShapeDtypeStruct((seq, ff), F32)),
        grid_spec=pltpu.PrefetchScalarGridSpec(
            num_scalar_prefetch=1,
            grid=(ff // WIDE,),
            in_specs=[
                pl.BlockSpec((2 * seq, block), lambda i, s: (0, s[21])),
                pl.BlockSpec((WIDE, block), lambda i, s: (i, 0)),
                small,
                wide,
                wide,
                pl.BlockSpec((WIDE, rank), lambda i, s: (i, 0)),
            ],
            out_specs=(small, wide),
        ),
    )(index, rows, mat, right, sums, act, proj)


def project(index, rows, mat, right, sums, acts, proj, left_all):
    seq, ff = sums.shape
    block, rank = mat.shape[1], proj.shape[1]
    half = rank // 2
    steps = ff // WIDE

    def kernel(s, rows_hbm, mat_ref, right_hbm, sum_hbm, near_hbm, act_f, proj_hbm, left_ref,
               out, rows_ref, right_n, sum_ref, act_n, proj_ref, sems):
        at = pl.multiple_of(s[23] * block, block)
        moves = [(rows_hbm.at[:, pl.ds(at, block)], rows_ref)]
        waits = []
        for k in range(steps):
            span = pl.ds(k * WIDE, WIDE)
            waits.append(len(moves))
            moves += [
                (near_hbm.at[:, span], act_n.at[:, span]),
                (proj_hbm.at[span], proj_ref.at[span]),
                (sum_hbm.at[:, span], sum_ref.at[:, span]),
            ]
            if k == 0:
                moves.append((right_hbm, right_n))
        waits.append(len(moves))
        copies = [
            pltpu.make_async_copy(source, target, sems.at[k])
            for k, (source, target) in enumerate(moves)
        ]
        for copy in copies:
            copy.start()
        copies[0].wait()
        sides = [None, None]
        for k in range(steps):
            for copy in copies[waits[k] : waits[k + 1]]:
                copy.wait()
            span = slice(k * WIDE, (k + 1) * WIDE)
            total = nt(rows_ref[...], mat_ref[span, :])
            hiddens = (total[:seq], sum_ref[:, span] + total[seq:])
            for i, (hidden, act) in enumerate(zip(hiddens, (act_n, act_f))):
                grad = (hidden * act[:, span].astype(F32)).astype(BF)
                term = jnp.dot(grad, proj_ref[span, :], preferred_element_type=F32)
                sides[i] = term if sides[i] is None else sides[i] + term
        sides[0] = sides[0] + right_n[...]
        pieces = []
        for z, side in ((s[0], sides[0]), (1 - s[0], sides[1])):
            left = sum(left_ref[4 * z + k].astype(F32) for k in range(4)).astype(BF)
            outer = jnp.dot(left, side.astype(BF), preferred_element_type=F32)
            pieces.append(jnp.concatenate([outer[:half], outer[half:]], axis=1).astype(BF))
        for copy in range(out.shape[0]):
            out[copy, :half, :] = pieces[0]
            out[copy, half:, :] = pieces[1]

    hbm = pl.BlockSpec(memory_space=pltpu.HBM)
    vmem = pl.BlockSpec(memory_space=pltpu.VMEM)
    mat, act_far, left_all = (
        pltpu.with_memory_space_constraint(v, pltpu.VMEM) for v in (mat, acts[1], left_all)
    )
    return pl.pallas_call(
        kernel,
        out_shape=jax.ShapeDtypeStruct((8, rank, 2 * rank), BF),
        in_specs=[pl.BlockSpec(memory_space=pltpu.SMEM), hbm, vmem, hbm, hbm, hbm, vmem, hbm, vmem],
        out_specs=vmem,
        scratch_shapes=[
            pltpu.VMEM((2 * seq, block), BF),
            pltpu.VMEM(right.shape, F32),
            pltpu.VMEM(sums.shape, F32),
            pltpu.VMEM(sums.shape, BF),
            pltpu.VMEM(proj.shape, BF),
            pltpu.SemaphoreType.DMA((2 + 3 * steps,)),
        ],
    )(index, rows, mat, right, sums, acts[0], act_far, proj, left_all)


def merge(parts):
    def kernel(ref, out):
        side = [
            [sum(ref[z, k, g].astype(F32) for k in range(4)) for g in range(2)] for z in range(2)
        ]
        first = (side[0][0] + side[1][1]).astype(BF)
        second = (side[1][0] + side[0][1]).astype(BF)
        for copy in range(out.shape[0]):
            out[copy, 0] = first
            out[copy, 1] = second

    parts = pltpu.with_memory_space_constraint(parts, pltpu.VMEM)
    return pl.pallas_call(
        kernel, out_shape=jax.ShapeDtypeStruct((32, 2) + parts.shape[3:], BF),
        in_specs=[pl.BlockSpec(memory_space=pltpu.VMEM)],
    )(parts)


def finish(me, parts, queries):
    rows, lanes = parts.shape[-2:]
    count, width = queries.shape
    examples = parts.shape[0] * parts.shape[2] * parts.shape[3]
    cuts = 4
    span = width // cuts

    def kernel(me_ref, ref, q_hbm, grads_ref, scores_ref, q_ref, table, sems):
        loads = [
            pltpu.make_async_copy(
                q_hbm.at[:, pl.ds(k * span, span)], q_ref.at[:, pl.ds(k * span, span)], sems.at[k]
            )
            for k in range(cuts)
        ]
        for load in loads:
            load.start()
        for y in range(4):
            for core in range(2):
                for z in range(2):
                    e = z * 8 + y * 2 + core
                    table[e * rows : (e + 1) * rows, :] = sum(
                        ref[y, k, core, z].astype(F32) for k in range(4)
                    )
        total = None
        for cut in range(cuts):
            loads[cut].wait()
            pieces = []
            for k in range(cut * rows // cuts, (cut + 1) * rows // cuts):
                pieces.append(table[pl.ds(k, examples, stride=rows), :].astype(BF))
                grads_ref[:, k * lanes : (k + 1) * lanes] = table[
                    pl.ds(me_ref[0] * rows + k, 1), :
                ]
            term = nt(
                jnp.concatenate(pieces, axis=1), q_ref[:, cut * span : (cut + 1) * span]
            )
            total = term if total is None else total + term
        scores_ref[...] = total

    hbm = pl.BlockSpec(memory_space=pltpu.HBM)
    vmem = pl.BlockSpec(memory_space=pltpu.VMEM)
    parts = pltpu.with_memory_space_constraint(parts, pltpu.VMEM)
    return pl.pallas_call(
        kernel,
        out_shape=(
            jax.ShapeDtypeStruct((1, rows * lanes), F32),
            jax.ShapeDtypeStruct((examples, count), F32),
        ),
        in_specs=[
            pl.BlockSpec(memory_space=pltpu.SMEM),
            vmem,
            hbm,
        ],
        out_specs=(vmem, vmem),
        scratch_shapes=[
            pltpu.VMEM(queries.shape, BF),
            pltpu.VMEM((examples * rows, lanes), F32),
            pltpu.SemaphoreType.DMA((cuts,)),
        ],
    )(me, parts, queries)


def along_y(v, forward):
    pairs = []
    for y in range(4):
        for core in range(2):
            step = 1 if (core == 0) == forward else 3
            pairs.append((2 * y + core, 2 * ((y + step) % 4) + core))
    return lax.ppermute(v, ("y", "c"), pairs)


def trade(copies, axes):
    return lax.all_to_all(copies, axes, 0, 0, tiled=True)


def on_device(inputs, gate_pre, up_out, weight, out_grad, seed_in, seed_out, queries):
    seq, block = out_grad.shape[0], weight.shape[1]
    rank = seed_in.shape[1]
    zh, y, c, zl, x = (lax.axis_index(name).astype(jnp.int32) for name in DP + TP)
    half = seq // 2

    w_one = along_y(weight, True)
    w_two = along_y(weight, False)
    m_own = flip(weight, "c")
    start = ((1 - zh) * 8 + ((y + x) % 4) * 2) * block
    odd = zl % 2
    far_a = lax.dynamic_slice(out_grad, (odd * half, start), (half, 2 * block))
    far_a = flip(far_a, "zh")
    far_b = lax.ppermute(far_a, "zl", [(0, 1), (1, 0), (2, 3), (3, 2)])

    proj = (seed_out.astype(F32) * 0.25 * (2.0 * FF) ** (-0.5)).astype(BF)
    gate = gate_pre.astype(F32)
    sigma = jax.nn.sigmoid(gate)
    act = (up_out.astype(F32) * sigma * (1.0 + gate * (1.0 - sigma))).astype(BF)
    one, two = jnp.where(c == 0, 3, 1), jnp.where(c == 0, 1, 3)
    slabs = [(0, c), (0, 1 - c), (one, c), (two, 1 - c), (two, c), (one, 1 - c), (2, c), (2, 1 - c)]
    index = [zh, x, odd, zh] + [zh * 8 + ((y + j) % 4) * 2 for j in range(4)]
    for j, core in slabs:
        index += [j, core]
    index = jnp.stack([jnp.asarray(v, jnp.int32) for v in index])
    act, proj, index = lax.optimization_barrier((act, proj, index))
    act_far = flip(act, "zh")

    order = jnp.concatenate([jnp.arange(0, rank, 2), jnp.arange(1, rank, 2)])
    pick = (jnp.arange(rank)[:, None] == order[None, :]).astype(BF)
    proj_in = (seed_in.astype(F32) * (2.0 * D) ** (-0.5)).astype(BF)
    proj_in = jnp.dot(proj_in, pick, preferred_element_type=F32).astype(BF)
    left = lax.dot_general(
        proj_in, inputs, (((0,), (1,)), ((), ())), preferred_element_type=F32
    ).astype(BF)
    left = sum(fetch(left, "x", s).astype(F32) for s in (1, 2, 3)) + left.astype(F32)
    left_all = everyone(left.astype(BF), ("zh", "zl"), 8)

    pieces_a = [far_a] + [fetch(far_a, "x", s) for s in (1, 2, 3)]
    pieces_b = [far_b] + [fetch(far_b, "x", s) for s in (1, 2, 3)]

    m_one = flip(w_one, "c")
    m_two = flip(w_two, "c")
    w_opp = along_y(w_one, True)
    m_opp = flip(w_opp, "c")

    mats = (weight, m_own, w_one, m_one, w_two, m_two)
    right, sums, rows = slab_sums(index, out_grad, pieces_a, pieces_b, mats, act, proj)
    right, sums = middle(index, rows, w_opp, right, sums, act, proj)
    payload = project(index, rows, m_opp, right, sums, (act, act_far), proj, left_all)
    z_all = trade(payload, ("zh", "zl"))
    merged = merge(z_all.reshape(2, 4, 2, rank // 2, 2 * rank))
    every = trade(merged, ("y", "x", "c"))
    me = (zh * 8 + y * 2 + c).reshape(1)
    every = every.reshape(4, 4, 2, 2, rank // 2, 2 * rank)
    return finish(me, every, queries)


def solution(mesh):
    fine = Mesh(mesh.devices.reshape(2, 4, 2, 4, 4), DP + TP)
    in_specs = (
        P(DP, TP),
        P(DP, TP),
        P(DP, TP),
        P(TP, DP),
        P(DP, None),
        P(TP, None),
        P(TP, None),
        P(DP + TP, None),
    )
    out_specs = (P(DP, None), P(None, DP + TP))

    return jax.shard_map(
        on_device, mesh=fine, in_specs=in_specs, out_specs=out_specs, check_vma=False
    )
```

time: 201 us -> 206 us (1.025)
  starting transfers between devices: 45.4 us -> 55.9 us
  local copies, waits for them, and re-layouts: 7.58 us -> 3.34 us
  Pallas kernels: 32.1 us -> 29 us
  waiting for transfers between devices: 98 us -> 95 us
  blocking collectives: 12.3 us -> 14.5 us
    all_to_all x1, waiting for transfers between devices: 6.19 us -> 19.8 us  [everyone(): return lax.all_to_all(copies, axes, 0, 0, tiled=True)]
    ppermute x6, waiting for transfers between devices: 18.8 us -> 7.11 us  [flip(): return lax.ppermute(v, axis, [(0, 1), (1, 0)])]
    ppermute x3, waiting for transfers between devices: 47.5 us -> 37.1 us  [along_y(): return lax.ppermute(v, ('y', 'c'), pairs)]
    ppermute x6 -> x9, waiting for transfers between devices: 14.1 us -> 19.6 us  [fetch(): return lax.ppermute(v, axis, [((i + step) % 4, i) for i in range(4)])]
    ppermute x0 -> x1, starting transfers between devices: none -> 5.36 us  [on_device(): far_b = lax.ppermute(far_a, 'zl', [(0, 1), (1, 0), (2, 3), (3, 2)])]
    unnamed x33 -> x23, local copies, waits for them, and re-layouts: 4.26 us -> 0.93 us
    ppermute x6 -> x9, starting transfers between devices: 4.16 us -> 6.59 us  [fetch(): return lax.ppermute(v, axis, [((i + step) % 4, i) for i in range(4)])]
    pallas_call x3, Pallas kernels: 27.3 us -> 25 us  [the longest x1 14.3 us: slab_sums(): pl.pallas_call(kernel, out_shape=(jax.ShapeDtypeStruct((seq, rank), F32),...]
  transfers between devices with their start and end apart: 17 -> 21, of which waited for: 8 -> 9; matrix products, arithmetic and copies ran while one was open for 5% -> 4% of each run, Pallas kernels for 10% -> 10%
where the time goes in v1:
time: 206 us; the launch traced here: 205 us
  waiting for transfers between devices  95 us (46%)
  starting transfers between devices  55.9 us (27%)
  Pallas kernels  29 us (14%)
  blocking collectives  14.5 us (7%)
  other arithmetic  4.91 us (2%)
  local copies, waits for them, and re-layouts  3.34 us (2%)
    ppermute x3, waiting for transfers between devices, along_y(): return lax.ppermute(v, ('y', 'c'), pairs)  37.1 us
    ppermute x6, starting transfers between devices, flip(): return lax.ppermute(v, axis, [(0, 1), (1, 0)])  23.8 us
    all_to_all x1, waiting for transfers between devices, everyone(): return lax.all_to_all(copies, axes, 0, 0, tiled=True)  19.8 us
    ppermute x9, waiting for transfers between devices, fetch(): return lax.ppermute(v, axis, [((i + step) % 4, i) for i in range(4)])  19.6 us
    all_to_all x1, blocking collectives, trade(): return lax.all_to_all(copies, axes, 0, 0, tiled=True)  14.5 us
    pallas_call x1, Pallas kernels, slab_sums(): pl.pallas_call(kernel, out_shape=(jax.ShapeDtypeStruct((seq, rank), F32),...  14.3 us
    all_to_all x1, waiting for transfers between devices, trade(): return lax.all_to_all(copies, axes, 0, 0, tiled=True)  11.4 us
    all_to_all x1, starting transfers between devices, trade(): return lax.all_to_all(copies, axes, 0, 0, tiled=True)  9.7 us
  transfers between devices with their start and end apart: 21, of which 9 were waited for; matrix products, arithmetic and copies ran while one was open for 4% of the time, Pallas kernels for 10%

profile of v1, /device:TPU:1, one launch (start us, length us, event | category | flops | bytes accessed | tf_op | source)
XLA Modules:
  0.0 205.1 jit_solution(9954589165247640385)
XLA Ops:
  0.6 3.6 %collective-permute-start.9 = (bf16[1792,512]{1,0:T(8,128)(2,1)}, bf16[1792,512]{1,0:T(8,128)(2,1)}, u32[]{:S(2)}, u32[]{:S(2)}) collective-permute-start(bf16[1792,512]{1,0:T(8,128)(2,1)} %refs_9_.1), channel_id=1, source_target_pairs={{0,32},{16,112},{32,64},{48,16},{64,96},{80,48},{96,0},{112,80},{1... | collective-permute-start | bytes 5505032 | tf_op jit(solution)/shard_map/ppermute | solution.py:299
  4.3 37.1 %collective-permute-done.9.refs_11_ = bf16[1792,512]{1,0:T(8,128)(2,1)} collective-permute-done((bf16[1792,512]{1,0:T(8,128)(2,1)}, bf16[1792,512]{1,0:T(8,128)(2,1)}, u32[]{:S(2)}, u32[]{:S(2)}) %collective-permute-start.9) | collective-permute-done | bytes 1835040 | tf_op jit(solution)/shard_map/ppermute | solution.py:299
  41.4 3.4 %collective-permute-start.13 = (bf16[1792,512]{1,0:T(8,128)(2,1)}, bf16[1792,512]{1,0:T(8,128)(2,1)}, u32[]{:S(2)}, u32[]{:S(2)}) collective-permute-start(bf16[1792,512]{1,0:T(8,128)(2,1)} %collective-permute-done.9.refs_11_), channel_id=1, source_target_pairs={{0,32},{16,112},{32,64},{48,16},{64,96},{80,48},{96,0},{112,80},{1... | collective-permute-start | bytes 5505032 | tf_op jit(solution)/shard_map/ppermute | solution.py:299
  44.8 1.0 dynamic_slice.3
  45.8 8.7 %collective-permute-start = (bf16[128,1024]{1,0:T(8,128)(2,1)S(1)}, bf16[128,1024]{1,0:T(8,128)(2,1)S(1)}, u32[]{:S(2)}, u32[]{:S(2)}) collective-permute-start(bf16[128,1024]{1,0:T(8,128)(2,1)S(1)} %dynamic_slice.3), channel_id=1, source_target_pairs={{0,128},{128,0},{1,129},{129,1},{2,130},{130,2},{3,131},{131,3},{4... | collective-permute-start | bytes 786440 | tf_op jit(solution)/shard_map/ppermute | solution.py:20
  54.6 7.1 %collective-permute-done.refs_1_ = bf16[128,1024]{1,0:T(8,128)(2,1)S(1)} collective-permute-done((bf16[128,1024]{1,0:T(8,128)(2,1)S(1)}, bf16[128,1024]{1,0:T(8,128)(2,1)S(1)}, u32[]{:S(2)}, u32[]{:S(2)}) %collective-permute-start) | collective-permute-done | bytes 262176 | tf_op jit(solution)/shard_map/ppermute | solution.py:20
  61.7 2.8 %collective-permute-start.1 = (bf16[128,1024]{1,0:T(8,128)(2,1)S(1)}, bf16[128,1024]{1,0:T(8,128)(2,1)S(1)}, u32[]{:S(2)}, u32[]{:S(2)}) collective-permute-start(bf16[128,1024]{1,0:T(8,128)(2,1)S(1)} %collective-permute-done.refs_1_), channel_id=1, source_target_pairs={{1,0},{2,1},{3,2},{0,3},{5,4},{6,5},{7,6},{4,7},{9,8},{10,9},{11,1... | collective-permute-start | bytes 786440 | tf_op jit(solution)/shard_map/ppermute | solution.py:24
  64.5 5.4 %collective-permute-start.4 = (bf16[128,1024]{1,0:T(8,128)(2,1)S(1)}, bf16[128,1024]{1,0:T(8,128)(2,1)}, u32[]{:S(2)}, u32[]{:S(2)}) collective-permute-start(bf16[128,1024]{1,0:T(8,128)(2,1)S(1)} %collective-permute-done.refs_1_), channel_id=1, source_target_pairs={{0,4},{4,0},{8,12},{12,8},{1,5},{5,1},{9,13},{13,9},{2,6},{6,2},{1... | collective-permute-start | bytes 786440 | tf_op jit(solution)/shard_map/ppermute | solution.py:319
  69.8 1.3 fusion.7
  71.3 4.0 %collective-permute-done.18 = bf16[64,256]{1,0:T(8,128)(2,1)S(1)} collective-permute-done((bf16[64,256]{1,0:T(8,128)(2,1)S(1)}, bf16[64,256]{1,0:T(8,128)(2,1)S(1)}, u32[]{:S(2)}, u32[]{:S(2)}) %collective-permute-start.18) | collective-permute-done | bytes 32800 | tf_op jit(solution)/shard_map/ppermute | solution.py:24
  75.2 4.3 %collective-permute-done.17 = bf16[64,256]{1,0:T(8,128)(2,1)S(1)} collective-permute-done((bf16[64,256]{1,0:T(8,128)(2,1)S(1)}, bf16[64,256]{1,0:T(8,128)(2,1)S(1)}, u32[]{:S(2)}, u32[]{:S(2)}) %collective-permute-start.17) | collective-permute-done | bytes 32800 | tf_op jit(solution)/shard_map/ppermute | solution.py:24
  80.1 2.5 %collective-permute-done.16 = bf16[64,256]{1,0:T(8,128)(2,1)} collective-permute-done((bf16[64,256]{1,0:T(8,128)(2,1)S(1)}, bf16[64,256]{1,0:T(8,128)(2,1)}, u32[]{:S(2)}, u32[]{:S(2)}) %collective-permute-start.16) | collective-permute-done | bytes 32800 | tf_op jit(solution)/shard_map/ppermute | solution.py:24
  82.6 1.6 collective-permute-start.3
  84.2 1.2 collective-permute-start.5
  85.3 4.1 %collective-permute-done.2.refs_3_ = bf16[128,1024]{1,0:T(8,128)(2,1)S(1)} collective-permute-done((bf16[128,1024]{1,0:T(8,128)(2,1)S(1)}, bf16[128,1024]{1,0:T(8,128)(2,1)S(1)}, u32[]{:S(2)}, u32[]{:S(2)}) %collective-permute-start.2) | collective-permute-done | bytes 262176 | tf_op jit(solution)/shard_map/ppermute | solution.py:24
  89.4 6.4 %collective-permute-start.8 = (bf16[1792,512]{1,0:T(8,128)(2,1)}, bf16[1792,512]{1,0:T(8,128)(2,1)}, u32[]{:S(2)}, u32[]{:S(2)}) collective-permute-start(bf16[1792,512]{1,0:T(8,128)(2,1)} %refs_9_.1), channel_id=1, source_target_pairs={{0,16},{16,0},{1,17},{17,1},{2,18},{18,2},{3,19},{19,3},{4,20},{20... | collective-permute-start | bytes 5505032 | tf_op jit(solution)/shard_map/ppermute | solution.py:20
  95.8 2.9 %collective-permute-start.10 = (bf16[1792,512]{1,0:T(8,128)(2,1)}, bf16[1792,512]{1,0:T(8,128)(2,1)}, u32[]{:S(2)}, u32[]{:S(2)}) collective-permute-start(bf16[1792,512]{1,0:T(8,128)(2,1)} %collective-permute-done.9.refs_11_), channel_id=1, source_target_pairs={{0,16},{16,0},{1,17},{17,1},{2,18},{18,2},{3,19},{19,3},{4,20},{20... | collective-permute-start | bytes 5505032 | tf_op jit(solution)/shard_map/ppermute | solution.py:20
  99.5 3.1 %fusion.5.refs_15_.act_ref.near_hbm = bf16[256,1792]{1,0:T(8,128)(2,1)} fusion(bf16[256,1792]{1,0:T(8,128)(2,1)} %param.9, bf16[256,1792]{1,0:T(8,128)(2,1)} %param.10), kind=kLoop, calls=%fused_computation.7 | loop fusion | flops 5046272 | bytes 2752512 | tf_op jit(solution)/shard_map/convert_element_type | solution.py:324
  103.7 0.9 collective-permute-start.7
  104.6 0.9 multiply_convert_fusion.refs_16_.proj_ref.proj_hbm
  105.5 4.8 %collective-permute-done.7.refs_8_ = bf16[128,1024]{1,0:T(8,128)(2,1)S(1)} collective-permute-done((bf16[128,1024]{1,0:T(8,128)(2,1)}, bf16[128,1024]{1,0:T(8,128)(2,1)S(1)}, u32[]{:S(2)}, u32[]{:S(2)}) %collective-permute-start.7) | collective-permute-done | bytes 262176 | tf_op jit(solution)/shard_map/ppermute | solution.py:24
  110.3 5.1 %collective-permute-start.15 = (bf16[256,1792]{1,0:T(8,128)(2,1)}, bf16[256,1792]{1,0:T(8,128)(2,1)S(1)}, u32[]{:S(2)}, u32[]{:S(2)}) collective-permute-start(bf16[256,1792]{1,0:T(8,128)(2,1)} %fusion.5.refs_15_.act_ref.near_hbm), channel_id=1, source_target_pairs={{0,128},{128,0},{1,129},{129,1},{2,130},{130,2},{3,131},{131,3},{4... | collective-permute-start | bytes 2752520 | tf_op jit(solution)/shard_map/ppermute | solution.py:20
  117.0 3.4 %all-to-all-start = ((bf16[8,64,256]{2,1,0:T(8,128)(2,1)}), bf16[8,64,256]{2,1,0:T(8,128)(2,1)S(1)}, u32[]{:S(2)}, u32[]{:S(2)}) async-start(bf16[8,64,256]{2,1,0:T(8,128)(2,1)} %broadcast_in_dim.2), calls=%async_computation | async-start | bytes 524288 | tf_op jit(solution)/shard_map/all_to_all | solution.py:29
  120.4 14.3 %shard_map.95 = (f32[256,64]{1,0:T(8,128)}, f32[256,1792]{1,0:T(8,128)}, bf16[512,1024]{1,0:T(8,128)(2,1)}) custom-call(s32[24]{0:T(128)} %stack.56.s._, bf16[256,8192]{1,0:T(8,128)(2,1)} %refs_0_.1, bf16[128,1024]{1,0:T(8,128)(2,1)} %copy-done.2, bf16[128,1024]{1,0:T(8,128)(2,1)} %copy-done.3, bf16[128,1024]{1,0:T(8,128)(2,1)} %copy-done.4, ...), custom_call_target="tpu_custom_call" | custom-call | tf_op jit(solution)/shard_map/pallas_call | solution.py:79
  134.7 5.5 %shard_map.96 = (f32[256,64]{1,0:T(8,128)}, f32[256,1792]{1,0:T(8,128)}) custom-call(s32[24]{0:T(128)} %stack.56.s._, bf16[512,1024]{1,0:T(8,128)(2,1)} %get-tuple-element.13.rows_ref.rows_hbm, bf16[1792,512]{1,0:T(8,128)(2,1)} %collective-permute-done.13.mat_ref, f32[256,64]{1,0:T(8,128)} %get-tuple-element.14.right_ref, ...), custom_call_target="tpu_custom_call" | custom-call | tf_op jit(solution)/shard_map/pallas_call | solution.py:124
  140.2 19.8 %all-to-all-done.left_ref = bf16[8,64,256]{2,1,0:T(8,128)(2,1)S(1)} async-done(((bf16[8,64,256]{2,1,0:T(8,128)(2,1)}), bf16[8,64,256]{2,1,0:T(8,128)(2,1)S(1)}, u32[]{:S(2)}, u32[]{:S(2)}) %all-to-all-start) | async-done | bytes 262176 | tf_op jit(solution)/shard_map/all_to_all | solution.py:29
  160.1 5.2 %shard_map.97 = bf16[8,64,128]{2,1,0:T(8,128)(2,1)} custom-call(s32[24]{0:T(128)} %stack.56.s._, bf16[512,1024]{1,0:T(8,128)(2,1)} %get-tuple-element.13.rows_ref.rows_hbm, bf16[1792,512]{1,0:T(8,128)(2,1)S(1)} %collective-permute-done.14.mat_ref, f32[256,64]{1,0:T(8,128)} %get-tuple-element.16.right_hbm, f32[256,1792]{1,0:T(8,128)} %get-tuple-element.17.sum_hbm, ...), custom_call_target="tpu_custom_call" | custom-call | tf_op jit(solution)/shard_map/pallas_call | solution.py:198
  165.2 14.5 %all_to_all.15 = bf16[8,64,128]{2,1,0:T(8,128)(2,1)S(1)} all-to-all(bf16[8,64,128]{2,1,0:T(8,128)(2,1)} %shard_map.97), channel_id=1, replica_groups=mesh['zh'=2,'y'=4,'c'=2,'zl'=4,'x'=4] {'zh','zl'}, dimensions={0} | all-to-all | bytes 262144 | tf_op jit(solution)/shard_map/all_to_all | solution.py:303
  179.7 0.9 shard_map.98
  180.6 9.7 %all-to-all-start.2 = ((bf16[32,2,32,128]{3,2,1,0:T(8,128)(2,1)}), bf16[32,2,32,128]{3,2,1,0:T(8,128)(2,1)S(1)}, u32[]{:S(2)}, u32[]{:S(2)}) async-start(bf16[32,2,32,128]{3,2,1,0:T(8,128)(2,1)} %shard_map.98), calls=%async_computation.2 | async-start | bytes 1048576 | tf_op jit(solution)/shard_map/all_to_all | solution.py:303
  190.3 11.4 %all-to-all-done.2 = bf16[32,2,32,128]{3,2,1,0:T(8,128)(2,1)S(1)} async-done(((bf16[32,2,32,128]{3,2,1,0:T(8,128)(2,1)}), bf16[32,2,32,128]{3,2,1,0:T(8,128)(2,1)S(1)}, u32[]{:S(2)}, u32[]{:S(2)}) %all-to-all-start.2) | async-done | bytes 524320 | tf_op jit(solution)/shard_map/all_to_all | solution.py:303
  201.7 3.2 %shard_map.99 = (f32[1,4096]{1,0:T(1,128)}, f32[16,256]{1,0:T(8,128)}) custom-call(s32[1]{0:T(128)} %bitcast.me_ref, bf16[4,4,2,2,32,128]{5,4,3,2,1,0:T(8,128)(2,1)S(1)} %bitcast.15, bf16[256,4096]{1,0:T(8,128)(2,1)} %q_hbm.1), custom_call_target="tpu_custom_call" | custom-call | tf_op jit(solution)/shard_map/pallas_call | solution.py:273
  (48 shorter events, 4.1 us)
Async XLA Ops:
  0.6 69.2 %copy-start = (bf16[256,512]{1,0:T(8,128)(2,1)S(1)}, bf16[256,512]{1,0:T(8,128)(2,1)}, u32[]{:S(2)}) copy-start(bf16[256,512]{1,0:T(8,128)(2,1)} %param.8) | copy-start | bytes 786436
  0.6 40.7 %collective-permute-start.9 = (bf16[1792,512]{1,0:T(8,128)(2,1)}, bf16[1792,512]{1,0:T(8,128)(2,1)}, u32[]{:S(2)}, u32[]{:S(2)}) collective-permute-start(bf16[1792,512]{1,0:T(8,128)(2,1)} %refs_9_.1), channel_id=1, source_target_pairs={{0,32},{16,112},{32,64},{48,16},{64,96},{80,48},{96,0},{112,80},{1... | collective-permute-start | bytes 5505032 | tf_op jit(solution)/shard_map/ppermute | solution.py:299
  4.3 94.4 %collective-permute-start.11 = (bf16[1792,512]{1,0:T(8,128)(2,1)}, bf16[1792,512]{1,0:T(8,128)(2,1)}, u32[]{:S(2)}, u32[]{:S(2)}) collective-permute-start(bf16[1792,512]{1,0:T(8,128)(2,1)} %refs_9_.1), channel_id=1, source_target_pairs={{0,96},{16,48},{32,0},{48,80},{64,32},{80,112},{96,64},{112,16},{1... | collective-permute-start | bytes 5505032 | tf_op jit(solution)/shard_map/ppermute | solution.py:299
  41.4 57.5 %collective-permute-start.13 = (bf16[1792,512]{1,0:T(8,128)(2,1)}, bf16[1792,512]{1,0:T(8,128)(2,1)}, u32[]{:S(2)}, u32[]{:S(2)}) collective-permute-start(bf16[1792,512]{1,0:T(8,128)(2,1)} %collective-permute-done.9.refs_11_), channel_id=1, source_target_pairs={{0,32},{16,112},{32,64},{48,16},{64,96},{80,48},{96,0},{112,80},{1... | collective-permute-start | bytes 5505032 | tf_op jit(solution)/shard_map/ppermute | solution.py:299
  44.8 57.9 %copy-start.1 = (s32[1792,64]{0,1:T(8,128)S(1)}, s32[1792,64]{0,1:T(8,128)}, u32[]{:S(2)}) copy-start(s32[1792,64]{0,1:T(8,128)} %param.14) | copy-start | bytes 1376260
  45.8 15.9 %collective-permute-start = (bf16[128,1024]{1,0:T(8,128)(2,1)S(1)}, bf16[128,1024]{1,0:T(8,128)(2,1)S(1)}, u32[]{:S(2)}, u32[]{:S(2)}) collective-permute-start(bf16[128,1024]{1,0:T(8,128)(2,1)S(1)} %dynamic_slice.3), channel_id=1, source_target_pairs={{0,128},{128,0},{1,129},{129,1},{2,130},{130,2},{3,131},{131,3},{4... | collective-permute-start | bytes 786440 | tf_op jit(solution)/shard_map/ppermute | solution.py:20
  61.7 37.1 %copy-start.2 = (bf16[128,1024]{1,0:T(8,128)(2,1)}, bf16[128,1024]{1,0:T(8,128)(2,1)S(1)}, u32[]{:S(2)}) copy-start(bf16[128,1024]{1,0:T(8,128)(2,1)S(1)} %collective-permute-done.refs_1_) | copy-start | bytes 786436
  61.7 20.9 %collective-permute-start.1 = (bf16[128,1024]{1,0:T(8,128)(2,1)S(1)}, bf16[128,1024]{1,0:T(8,128)(2,1)S(1)}, u32[]{:S(2)}, u32[]{:S(2)}) collective-permute-start(bf16[128,1024]{1,0:T(8,128)(2,1)S(1)} %collective-permute-done.refs_1_), channel_id=1, source_target_pairs={{1,0},{2,1},{3,2},{0,3},{5,4},{6,5},{7,6},{4,7},{9,8},{10,9},{11,1... | collective-permute-start | bytes 786440 | tf_op jit(solution)/shard_map/ppermute | solution.py:24
  64.5 19.7 %collective-permute-start.4 = (bf16[128,1024]{1,0:T(8,128)(2,1)S(1)}, bf16[128,1024]{1,0:T(8,128)(2,1)}, u32[]{:S(2)}, u32[]{:S(2)}) collective-permute-start(bf16[128,1024]{1,0:T(8,128)(2,1)S(1)} %collective-permute-done.refs_1_), channel_id=1, source_target_pairs={{0,4},{4,0},{8,12},{12,8},{1,5},{5,1},{9,13},{13,9},{2,6},{6,2},{1... | collective-permute-start | bytes 786440 | tf_op jit(solution)/shard_map/ppermute | solution.py:319
  71.2 8.3 %copy-start.8 = (bf16[64,256]{1,0:T(8,128)(2,1)}, bf16[64,256]{1,0:T(8,128)(2,1)S(1)}, u32[]{:S(2)}) copy-start(bf16[64,256]{1,0:T(8,128)(2,1)S(1)} %fusion.7) | copy-start | bytes 98308
  71.2 4.1 %collective-permute-start.18 = (bf16[64,256]{1,0:T(8,128)(2,1)S(1)}, bf16[64,256]{1,0:T(8,128)(2,1)S(1)}, u32[]{:S(2)}, u32[]{:S(2)}) collective-permute-start(bf16[64,256]{1,0:T(8,128)(2,1)S(1)} %fusion.7), channel_id=1, source_target_pairs={{3,0},{0,1},{1,2},{2,3},{7,4},{4,5},{5,6},{6,7},{11,8},{8,9},{9,10... | collective-permute-start | bytes 98312 | tf_op jit(solution)/shard_map/ppermute | solution.py:24
  75.2 4.3 %copy-start.9 = (bf16[64,256]{1,0:T(8,128)(2,1)}, bf16[64,256]{1,0:T(8,128)(2,1)S(1)}, u32[]{:S(2)}) copy-start(bf16[64,256]{1,0:T(8,128)(2,1)S(1)} %collective-permute-done.18) | copy-start | bytes 98308
  75.2 4.3 %collective-permute-start.17 = (bf16[64,256]{1,0:T(8,128)(2,1)S(1)}, bf16[64,256]{1,0:T(8,128)(2,1)S(1)}, u32[]{:S(2)}, u32[]{:S(2)}) collective-permute-start(bf16[64,256]{1,0:T(8,128)(2,1)S(1)} %fusion.7), channel_id=1, source_target_pairs={{2,0},{3,1},{0,2},{1,3},{6,4},{7,5},{4,6},{5,7},{10,8},{11,9},{8,1... | collective-permute-start | bytes 98312 | tf_op jit(solution)/shard_map/ppermute | solution.py:24
  79.5 0.6 copy-start.10
  79.5 3.1 %collective-permute-start.16 = (bf16[64,256]{1,0:T(8,128)(2,1)S(1)}, bf16[64,256]{1,0:T(8,128)(2,1)}, u32[]{:S(2)}, u32[]{:S(2)}) collective-permute-start(bf16[64,256]{1,0:T(8,128)(2,1)S(1)} %fusion.7), channel_id=1, source_target_pairs={{1,0},{2,1},{3,2},{0,3},{5,4},{6,5},{7,6},{4,7},{9,8},{10,9},{11,1... | collective-permute-start | bytes 98312 | tf_op jit(solution)/shard_map/ppermute | solution.py:24
  82.6 6.8 %collective-permute-start.2 = (bf16[128,1024]{1,0:T(8,128)(2,1)S(1)}, bf16[128,1024]{1,0:T(8,128)(2,1)S(1)}, u32[]{:S(2)}, u32[]{:S(2)}) collective-permute-start(bf16[128,1024]{1,0:T(8,128)(2,1)S(1)} %collective-permute-done.refs_1_), channel_id=1, source_target_pairs={{2,0},{3,1},{0,2},{1,3},{6,4},{7,5},{4,6},{5,7},{10,8},{11,9},{8,1... | collective-permute-start | bytes 786440 | tf_op jit(solution)/shard_map/ppermute | solution.py:24
  82.6 16.2 %copy-start.3 = (bf16[128,1024]{1,0:T(8,128)(2,1)}, bf16[128,1024]{1,0:T(8,128)(2,1)S(1)}, u32[]{:S(2)}) copy-start(bf16[128,1024]{1,0:T(8,128)(2,1)S(1)} %collective-permute-done.1.refs_2_) | copy-start | bytes 786436
  82.6 13.2 %collective-permute-start.3 = (bf16[128,1024]{1,0:T(8,128)(2,1)S(1)}, bf16[128,1024]{1,0:T(8,128)(2,1)S(1)}, u32[]{:S(2)}, u32[]{:S(2)}) collective-permute-start(bf16[128,1024]{1,0:T(8,128)(2,1)S(1)} %collective-permute-done.refs_1_), channel_id=1, source_target_pairs={{3,0},{0,1},{1,2},{2,3},{7,4},{4,5},{5,6},{6,7},{11,8},{8,9},{9,10... | collective-permute-start | bytes 786440 | tf_op jit(solution)/shard_map/ppermute | solution.py:24
  84.2 11.6 %collective-permute-start.5 = (bf16[128,1024]{1,0:T(8,128)(2,1)}, bf16[128,1024]{1,0:T(8,128)(2,1)S(1)}, u32[]{:S(2)}, u32[]{:S(2)}) collective-permute-start(bf16[128,1024]{1,0:T(8,128)(2,1)} %collective-permute-done.4.refs_5_), channel_id=1, source_target_pairs={{1,0},{2,1},{3,2},{0,3},{5,4},{6,5},{7,6},{4,7},{9,8},{10,9},{11,1... | collective-permute-start | bytes 786440 | tf_op jit(solution)/shard_map/ppermute | solution.py:24
  89.4 9.4 %copy-start.4 = (bf16[128,1024]{1,0:T(8,128)(2,1)}, bf16[128,1024]{1,0:T(8,128)(2,1)S(1)}, u32[]{:S(2)}) copy-start(bf16[128,1024]{1,0:T(8,128)(2,1)S(1)} %collective-permute-done.2.refs_3_) | copy-start | bytes 786436
  89.4 31.0 %collective-permute-start.8 = (bf16[1792,512]{1,0:T(8,128)(2,1)}, bf16[1792,512]{1,0:T(8,128)(2,1)}, u32[]{:S(2)}, u32[]{:S(2)}) collective-permute-start(bf16[1792,512]{1,0:T(8,128)(2,1)} %refs_9_.1), channel_id=1, source_target_pairs={{0,16},{16,0},{1,17},{17,1},{2,18},{18,2},{3,19},{19,3},{4,20},{20... | collective-permute-start | bytes 5505032 | tf_op jit(solution)/shard_map/ppermute | solution.py:20
  95.8 3.1 %copy-start.5 = (bf16[128,1024]{1,0:T(8,128)(2,1)}, bf16[128,1024]{1,0:T(8,128)(2,1)S(1)}, u32[]{:S(2)}) copy-start(bf16[128,1024]{1,0:T(8,128)(2,1)S(1)} %collective-permute-done.3.refs_4_) | copy-start | bytes 786436
  95.8 7.9 %collective-permute-start.6 = (bf16[128,1024]{1,0:T(8,128)(2,1)}, bf16[128,1024]{1,0:T(8,128)(2,1)}, u32[]{:S(2)}, u32[]{:S(2)}) collective-permute-start(bf16[128,1024]{1,0:T(8,128)(2,1)} %collective-permute-done.4.refs_5_), channel_id=1, source_target_pairs={{2,0},{3,1},{0,2},{1,3},{6,4},{7,5},{4,6},{5,7},{10,8},{11,9},{8,1... | collective-permute-start | bytes 786440 | tf_op jit(solution)/shard_map/ppermute | solution.py:24
  95.8 3.0 %copy-start.6 = (bf16[128,1024]{1,0:T(8,128)(2,1)}, bf16[128,1024]{1,0:T(8,128)(2,1)S(1)}, u32[]{:S(2)}) copy-start(bf16[128,1024]{1,0:T(8,128)(2,1)S(1)} %collective-permute-done.5.refs_6_) | copy-start | bytes 786436
  95.8 24.6 %collective-permute-start.10 = (bf16[1792,512]{1,0:T(8,128)(2,1)}, bf16[1792,512]{1,0:T(8,128)(2,1)}, u32[]{:S(2)}, u32[]{:S(2)}) collective-permute-start(bf16[1792,512]{1,0:T(8,128)(2,1)} %collective-permute-done.9.refs_11_), channel_id=1, source_target_pairs={{0,16},{16,0},{1,17},{17,1},{2,18},{18,2},{3,19},{19,3},{4,20},{20... | collective-permute-start | bytes 5505032 | tf_op jit(solution)/shard_map/ppermute | solution.py:20
  98.7 21.7 %collective-permute-start.12 = (bf16[1792,512]{1,0:T(8,128)(2,1)}, bf16[1792,512]{1,0:T(8,128)(2,1)}, u32[]{:S(2)}, u32[]{:S(2)}) collective-permute-start(bf16[1792,512]{1,0:T(8,128)(2,1)} %collective-permute-done.11.refs_13_), channel_id=1, source_target_pairs={{0,16},{16,0},{1,17},{17,1},{2,18},{18,2},{3,19},{19,3},{4,20},{20... | collective-permute-start | bytes 5505032 | tf_op jit(solution)/shard_map/ppermute | solution.py:20
  98.8 61.2 %collective-permute-start.14 = (bf16[1792,512]{1,0:T(8,128)(2,1)}, bf16[1792,512]{1,0:T(8,128)(2,1)S(1)}, u32[]{:S(2)}, u32[]{:S(2)}) collective-permute-start(bf16[1792,512]{1,0:T(8,128)(2,1)} %collective-permute-done.13.mat_ref), channel_id=1, source_target_pairs={{0,16},{16,0},{1,17},{17,1},{2,18},{18,2},{3,19},{19,3},{4,20},{20... | collective-permute-start | bytes 5505032 | tf_op jit(solution)/shard_map/ppermute | solution.py:20
  103.7 6.6 %collective-permute-start.7 = (bf16[128,1024]{1,0:T(8,128)(2,1)}, bf16[128,1024]{1,0:T(8,128)(2,1)S(1)}, u32[]{:S(2)}, u32[]{:S(2)}) collective-permute-start(bf16[128,1024]{1,0:T(8,128)(2,1)} %collective-permute-done.4.refs_5_), channel_id=1, source_target_pairs={{3,0},{0,1},{1,2},{2,3},{7,4},{4,5},{5,6},{6,7},{11,8},{8,9},{9,10... | collective-permute-start | bytes 786440 | tf_op jit(solution)/shard_map/ppermute | solution.py:24
  110.3 10.1 %copy-start.7 = (bf16[128,1024]{1,0:T(8,128)(2,1)}, bf16[128,1024]{1,0:T(8,128)(2,1)S(1)}, u32[]{:S(2)}) copy-start(bf16[128,1024]{1,0:T(8,128)(2,1)S(1)} %collective-permute-done.7.refs_8_) | copy-start | bytes 786436
  110.3 49.8 %collective-permute-start.15 = (bf16[256,1792]{1,0:T(8,128)(2,1)}, bf16[256,1792]{1,0:T(8,128)(2,1)S(1)}, u32[]{:S(2)}, u32[]{:S(2)}) collective-permute-start(bf16[256,1792]{1,0:T(8,128)(2,1)} %fusion.5.refs_15_.act_ref.near_hbm), channel_id=1, source_target_pairs={{0,128},{128,0},{1,129},{129,1},{2,130},{130,2},{3,131},{131,3},{4... | collective-permute-start | bytes 2752520 | tf_op jit(solution)/shard_map/ppermute | solution.py:20
  117.0 43.1 %all-to-all-start = ((bf16[8,64,256]{2,1,0:T(8,128)(2,1)}), bf16[8,64,256]{2,1,0:T(8,128)(2,1)S(1)}, u32[]{:S(2)}, u32[]{:S(2)}) async-start(bf16[8,64,256]{2,1,0:T(8,128)(2,1)} %broadcast_in_dim.2), calls=%async_computation | async-start | bytes 524288 | tf_op jit(solution)/shard_map/all_to_all | solution.py:29
  180.6 21.1 %all-to-all-start.2 = ((bf16[32,2,32,128]{3,2,1,0:T(8,128)(2,1)}), bf16[32,2,32,128]{3,2,1,0:T(8,128)(2,1)S(1)}, u32[]{:S(2)}, u32[]{:S(2)}) async-start(bf16[32,2,32,128]{3,2,1,0:T(8,128)(2,1)} %shard_map.98), calls=%async_computation.2 | async-start | bytes 1048576 | tf_op jit(solution)/shard_map/all_to_all | solution.py:303

commit v2 on v1

--- a/solution.py
+++ b/solution.py
@@ -146,8 +146,8 @@
     half = rank // 2
     steps = ff // WIDE
 
-    def kernel(s, rows_hbm, mat_ref, right_hbm, sum_hbm, near_hbm, act_f, proj_hbm, left_ref,
-               out, rows_ref, right_n, sum_ref, act_n, proj_ref, sems):
+    def kernel(s, rows_hbm, mat_hbm, right_hbm, sum_hbm, near_hbm, far_hbm, proj_hbm, left_hbm,
+               out, rows_ref, mat_ref, right_n, sum_ref, act_n, act_f, proj_ref, left_ref, sems):
         at = pl.multiple_of(s[23] * block, block)
         moves = [(rows_hbm.at[:, pl.ds(at, block)], rows_ref)]
         waits = []
@@ -155,13 +155,16 @@
             span = pl.ds(k * WIDE, WIDE)
             waits.append(len(moves))
             moves += [
+                (mat_hbm.at[span], mat_ref.at[span]),
                 (near_hbm.at[:, span], act_n.at[:, span]),
                 (proj_hbm.at[span], proj_ref.at[span]),
                 (sum_hbm.at[:, span], sum_ref.at[:, span]),
+                (far_hbm.at[:, span], act_f.at[:, span]),
             ]
             if k == 0:
                 moves.append((right_hbm, right_n))
         waits.append(len(moves))
+        moves.append((left_hbm, left_ref))
         copies = [
             pltpu.make_async_copy(source, target, sems.at[k])
             for k, (source, target) in enumerate(moves)
@@ -181,6 +184,7 @@
                 term = jnp.dot(grad, proj_ref[span, :], preferred_element_type=F32)
                 sides[i] = term if sides[i] is None else sides[i] + term
         sides[0] = sides[0] + right_n[...]
+        copies[-1].wait()
         pieces = []
         for z, side in ((s[0], sides[0]), (1 - s[0], sides[1])):
             left = sum(left_ref[4 * z + k].astype(F32) for k in range(4)).astype(BF)
@@ -191,24 +195,23 @@
             out[copy, half:, :] = pieces[1]
 
     hbm = pl.BlockSpec(memory_space=pltpu.HBM)
-    vmem = pl.BlockSpec(memory_space=pltpu.VMEM)
-    mat, act_far, left_all = (
-        pltpu.with_memory_space_constraint(v, pltpu.VMEM) for v in (mat, acts[1], left_all)
-    )
     return pl.pallas_call(
         kernel,
         out_shape=jax.ShapeDtypeStruct((8, rank, 2 * rank), BF),
-        in_specs=[pl.BlockSpec(memory_space=pltpu.SMEM), hbm, vmem, hbm, hbm, hbm, vmem, hbm, vmem],
-        out_specs=vmem,
+        in_specs=[pl.BlockSpec(memory_space=pltpu.SMEM)] + [hbm] * 8,
+        out_specs=pl.BlockSpec(memory_space=pltpu.VMEM),
         scratch_shapes=[
             pltpu.VMEM((2 * seq, block), BF),
+            pltpu.VMEM(mat.shape, BF),
             pltpu.VMEM(right.shape, F32),
             pltpu.VMEM(sums.shape, F32),
             pltpu.VMEM(sums.shape, BF),
+            pltpu.VMEM(sums.shape, BF),
             pltpu.VMEM(proj.shape, BF),
-            pltpu.SemaphoreType.DMA((2 + 3 * steps,)),
+            pltpu.VMEM(left_all.shape, BF),
+            pltpu.SemaphoreType.DMA((3 + 5 * steps,)),
         ],
-    )(index, rows, mat, right, sums, acts[0], act_far, proj, left_all)
+    )(index, rows, mat, right, sums, *acts, proj, left_all)
 
 
 def merge(parts):

time: 206 us -> 206 us (level)
    all_to_all x1, starting transfers between devices: 9.7 us -> 6.38 us  [trade(): return lax.all_to_all(copies, axes, 0, 0, tiled=True)]
where the time goes in v2:
time: 206 us; the launch traced here: 205 us
  waiting for transfers between devices  96.3 us (47%)
  starting transfers between devices  54.7 us (27%)
  Pallas kernels  29.5 us (14%)
  blocking collectives  15 us (7%)
  local copies, waits for them, and re-layouts  3.83 us (2%)
  other arithmetic  3.18 us (2%)
    ppermute x3, waiting for transfers between devices, along_y(): return lax.ppermute(v, ('y', 'c'), pairs)  37.1 us
    ppermute x6, starting transfers between devices, flip(): return lax.ppermute(v, axis, [(0, 1), (1, 0)])  24.2 us
    all_to_all x1, waiting for transfers between devices, everyone(): return lax.all_to_all(copies, axes, 0, 0, tiled=True)  20.8 us
    ppermute x9, waiting for transfers between devices, fetch(): return lax.ppermute(v, axis, [((i + step) % 4, i) for i in range(4)])  20 us
    all_to_all x1, blocking collectives, trade(): return lax.all_to_all(copies, axes, 0, 0, tiled=True)  15 us
    pallas_call x1, Pallas kernels, slab_sums(): pl.pallas_call(kernel, out_shape=(jax.ShapeDtypeStruct((seq, rank), F32),...  14.2 us
    all_to_all x1, waiting for transfers between devices, trade(): return lax.all_to_all(copies, axes, 0, 0, tiled=True)  11.4 us
    ppermute x6, waiting for transfers between devices, flip(): return lax.ppermute(v, axis, [(0, 1), (1, 0)])  7.11 us
  transfers between devices with their start and end apart: 21, of which 9 were waited for; matrix products, arithmetic and copies ran while one was open for 4% of the time, Pallas kernels for 10%

profile of v2, /device:TPU:1, one launch (start us, length us, event | category | flops | bytes accessed | tf_op | source)
XLA Modules:
  0.0 205.0 jit_solution(11959162759066257799)
XLA Ops:
  0.6 3.6 %collective-permute-start.9 = (bf16[1792,512]{1,0:T(8,128)(2,1)}, bf16[1792,512]{1,0:T(8,128)(2,1)}, u32[]{:S(2)}, u32[]{:S(2)}) collective-permute-start(bf16[1792,512]{1,0:T(8,128)(2,1)} %refs_9_.1), channel_id=1, source_target_pairs={{0,32},{16,112},{32,64},{48,16},{64,96},{80,48},{96,0},{112,80},{1... | collective-permute-start | bytes 5505032 | tf_op jit(solution)/shard_map/ppermute | solution.py:302
  4.3 37.1 %collective-permute-done.9.refs_11_ = bf16[1792,512]{1,0:T(8,128)(2,1)} collective-permute-done((bf16[1792,512]{1,0:T(8,128)(2,1)}, bf16[1792,512]{1,0:T(8,128)(2,1)}, u32[]{:S(2)}, u32[]{:S(2)}) %collective-permute-start.9) | collective-permute-done | bytes 1835040 | tf_op jit(solution)/shard_map/ppermute | solution.py:302
  41.4 3.4 %collective-permute-start.13 = (bf16[1792,512]{1,0:T(8,128)(2,1)}, bf16[1792,512]{1,0:T(8,128)(2,1)}, u32[]{:S(2)}, u32[]{:S(2)}) collective-permute-start(bf16[1792,512]{1,0:T(8,128)(2,1)} %collective-permute-done.9.refs_11_), channel_id=1, source_target_pairs={{0,32},{16,112},{32,64},{48,16},{64,96},{80,48},{96,0},{112,80},{1... | collective-permute-start | bytes 5505032 | tf_op jit(solution)/shard_map/ppermute | solution.py:302
  44.8 1.0 dynamic_slice.3
  45.8 8.7 %collective-permute-start = (bf16[128,1024]{1,0:T(8,128)(2,1)S(1)}, bf16[128,1024]{1,0:T(8,128)(2,1)S(1)}, u32[]{:S(2)}, u32[]{:S(2)}) collective-permute-start(bf16[128,1024]{1,0:T(8,128)(2,1)S(1)} %dynamic_slice.3), channel_id=1, source_target_pairs={{0,128},{128,0},{1,129},{129,1},{2,130},{130,2},{3,131},{131,3},{4... | collective-permute-start | bytes 786440 | tf_op jit(solution)/shard_map/ppermute | solution.py:20
  54.6 7.1 %collective-permute-done.refs_1_ = bf16[128,1024]{1,0:T(8,128)(2,1)S(1)} collective-permute-done((bf16[128,1024]{1,0:T(8,128)(2,1)S(1)}, bf16[128,1024]{1,0:T(8,128)(2,1)S(1)}, u32[]{:S(2)}, u32[]{:S(2)}) %collective-permute-start) | collective-permute-done | bytes 262176 | tf_op jit(solution)/shard_map/ppermute | solution.py:20
  61.7 2.8 %collective-permute-start.1 = (bf16[128,1024]{1,0:T(8,128)(2,1)S(1)}, bf16[128,1024]{1,0:T(8,128)(2,1)S(1)}, u32[]{:S(2)}, u32[]{:S(2)}) collective-permute-start(bf16[128,1024]{1,0:T(8,128)(2,1)S(1)} %collective-permute-done.refs_1_), channel_id=1, source_target_pairs={{1,0},{2,1},{3,2},{0,3},{5,4},{6,5},{7,6},{4,7},{9,8},{10,9},{11,1... | collective-permute-start | bytes 786440 | tf_op jit(solution)/shard_map/ppermute | solution.py:24
  64.5 5.4 %collective-permute-start.4 = (bf16[128,1024]{1,0:T(8,128)(2,1)S(1)}, bf16[128,1024]{1,0:T(8,128)(2,1)S(1)}, u32[]{:S(2)}, u32[]{:S(2)}) collective-permute-start(bf16[128,1024]{1,0:T(8,128)(2,1)S(1)} %collective-permute-done.refs_1_), channel_id=1, source_target_pairs={{0,4},{4,0},{8,12},{12,8},{1,5},{5,1},{9,13},{13,9},{2,6},{6,2},{1... | collective-permute-start | bytes 786440 | tf_op jit(solution)/shard_map/ppermute | solution.py:322
  69.8 1.3 fusion.7
  71.3 4.0 %collective-permute-done.18 = bf16[64,256]{1,0:T(8,128)(2,1)S(1)} collective-permute-done((bf16[64,256]{1,0:T(8,128)(2,1)S(1)}, bf16[64,256]{1,0:T(8,128)(2,1)S(1)}, u32[]{:S(2)}, u32[]{:S(2)}) %collective-permute-start.18) | collective-permute-done | bytes 32800 | tf_op jit(solution)/shard_map/ppermute | solution.py:24
  75.2 4.3 %collective-permute-done.17 = bf16[64,256]{1,0:T(8,128)(2,1)S(1)} collective-permute-done((bf16[64,256]{1,0:T(8,128)(2,1)S(1)}, bf16[64,256]{1,0:T(8,128)(2,1)S(1)}, u32[]{:S(2)}, u32[]{:S(2)}) %collective-permute-start.17) | collective-permute-done | bytes 32800 | tf_op jit(solution)/shard_map/ppermute | solution.py:24
  79.5 3.1 %collective-permute-done.16 = bf16[64,256]{1,0:T(8,128)(2,1)S(1)} collective-permute-done((bf16[64,256]{1,0:T(8,128)(2,1)S(1)}, bf16[64,256]{1,0:T(8,128)(2,1)S(1)}, u32[]{:S(2)}, u32[]{:S(2)}) %collective-permute-start.16) | collective-permute-done | bytes 32800 | tf_op jit(solution)/shard_map/ppermute | solution.py:24
  82.6 1.5 collective-permute-start.3
  84.1 1.3 collective-permute-start.5
  85.3 4.1 %collective-permute-done.2.refs_3_ = bf16[128,1024]{1,0:T(8,128)(2,1)S(1)} collective-permute-done((bf16[128,1024]{1,0:T(8,128)(2,1)S(1)}, bf16[128,1024]{1,0:T(8,128)(2,1)S(1)}, u32[]{:S(2)}, u32[]{:S(2)}) %collective-permute-start.2) | collective-permute-done | bytes 262176 | tf_op jit(solution)/shard_map/ppermute | solution.py:24
  89.4 6.4 %collective-permute-start.8 = (bf16[1792,512]{1,0:T(8,128)(2,1)}, bf16[1792,512]{1,0:T(8,128)(2,1)}, u32[]{:S(2)}, u32[]{:S(2)}) collective-permute-start(bf16[1792,512]{1,0:T(8,128)(2,1)} %refs_9_.1), channel_id=1, source_target_pairs={{0,16},{16,0},{1,17},{17,1},{2,18},{18,2},{3,19},{19,3},{4,20},{20... | collective-permute-start | bytes 5505032 | tf_op jit(solution)/shard_map/ppermute | solution.py:20
  95.8 2.9 %collective-permute-start.10 = (bf16[1792,512]{1,0:T(8,128)(2,1)}, bf16[1792,512]{1,0:T(8,128)(2,1)}, u32[]{:S(2)}, u32[]{:S(2)}) collective-permute-start(bf16[1792,512]{1,0:T(8,128)(2,1)} %collective-permute-done.9.refs_11_), channel_id=1, source_target_pairs={{0,16},{16,0},{1,17},{17,1},{2,18},{18,2},{3,19},{19,3},{4,20},{20... | collective-permute-start | bytes 5505032 | tf_op jit(solution)/shard_map/ppermute | solution.py:20
  99.5 2.2 %fusion.5.refs_15_.act_ref.near_hbm = bf16[256,1792]{1,0:T(8,128)(2,1)S(1)} fusion(bf16[256,1792]{1,0:T(8,128)(2,1)} %param.9, bf16[256,1792]{1,0:T(8,128)(2,1)} %param.10), kind=kLoop, calls=%fused_computation.7 | loop fusion | flops 5046272 | bytes 2752512 | tf_op jit(solution)/shard_map/convert_element_type | solution.py:327
  102.8 0.9 collective-permute-start.7
  103.8 0.9 multiply_convert_fusion.refs_16_.proj_ref.proj_hbm
  104.7 4.6 %collective-permute-done.7.refs_8_ = bf16[128,1024]{1,0:T(8,128)(2,1)S(1)} collective-permute-done((bf16[128,1024]{1,0:T(8,128)(2,1)S(1)}, bf16[128,1024]{1,0:T(8,128)(2,1)S(1)}, u32[]{:S(2)}, u32[]{:S(2)}) %collective-permute-start.7) | collective-permute-done | bytes 262176 | tf_op jit(solution)/shard_map/ppermute | solution.py:24
  109.3 5.4 %collective-permute-start.15 = (bf16[256,1792]{1,0:T(8,128)(2,1)S(1)}, bf16[256,1792]{1,0:T(8,128)(2,1)S(1)}, u32[]{:S(2)}, u32[]{:S(2)}) collective-permute-start(bf16[256,1792]{1,0:T(8,128)(2,1)S(1)} %fusion.5.refs_15_.act_ref.near_hbm), channel_id=1, source_target_pairs={{0,128},{128,0},{1,129},{129,1},{2,130},{130,2},{3,131},{131,3},{4... | collective-permute-start | bytes 2752520 | tf_op jit(solution)/shard_map/ppermute | solution.py:20
  115.4 5.2 %all-to-all-start = ((bf16[8,64,256]{2,1,0:T(8,128)(2,1)}), bf16[8,64,256]{2,1,0:T(8,128)(2,1)S(1)}, u32[]{:S(2)}, u32[]{:S(2)}) async-start(bf16[8,64,256]{2,1,0:T(8,128)(2,1)} %broadcast_in_dim.2), calls=%async_computation | async-start | bytes 524288 | tf_op jit(solution)/shard_map/all_to_all | solution.py:29
  120.7 14.2 %shard_map.95 = (f32[256,64]{1,0:T(8,128)}, f32[256,1792]{1,0:T(8,128)}, bf16[512,1024]{1,0:T(8,128)(2,1)}) custom-call(s32[24]{0:T(128)} %stack.56.s._, bf16[256,8192]{1,0:T(8,128)(2,1)} %refs_0_.1, bf16[128,1024]{1,0:T(8,128)(2,1)} %copy-done.5, bf16[128,1024]{1,0:T(8,128)(2,1)} %copy-done.6, bf16[128,1024]{1,0:T(8,128)(2,1)} %copy-done.8, ...), custom_call_target="tpu_custom_call" | custom-call | tf_op jit(solution)/shard_map/pallas_call | solution.py:79
  134.9 5.5 %shard_map.96 = (f32[256,64]{1,0:T(8,128)}, f32[256,1792]{1,0:T(8,128)}) custom-call(s32[24]{0:T(128)} %stack.56.s._, bf16[512,1024]{1,0:T(8,128)(2,1)} %get-tuple-element.13.rows_ref.rows_hbm, bf16[1792,512]{1,0:T(8,128)(2,1)} %collective-permute-done.13.mat_ref, f32[256,64]{1,0:T(8,128)} %get-tuple-element.14.right_ref, ...), custom_call_target="tpu_custom_call" | custom-call | tf_op jit(solution)/shard_map/pallas_call | solution.py:124
  140.4 20.8 %all-to-all-done.left_hbm = bf16[8,64,256]{2,1,0:T(8,128)(2,1)S(1)} async-done(((bf16[8,64,256]{2,1,0:T(8,128)(2,1)}), bf16[8,64,256]{2,1,0:T(8,128)(2,1)S(1)}, u32[]{:S(2)}, u32[]{:S(2)}) %all-to-all-start) | async-done | bytes 262176 | tf_op jit(solution)/shard_map/all_to_all | solution.py:29
  162.2 5.8 %shard_map.97 = bf16[8,64,128]{2,1,0:T(8,128)(2,1)} custom-call(s32[24]{0:T(128)} %stack.56.s._, bf16[512,1024]{1,0:T(8,128)(2,1)} %get-tuple-element.13.rows_ref.rows_hbm, bf16[1792,512]{1,0:T(8,128)(2,1)} %collective-permute-done.14.mat_hbm, f32[256,64]{1,0:T(8,128)} %get-tuple-element.16.right_hbm, f32[256,1792]{1,0:T(8,128)} %get-tuple-element.17.sum_hbm, ...), custom_call_target="tpu_custom_call" | custom-call | tf_op jit(solution)/shard_map/pallas_call | solution.py:198
  168.0 15.0 %all_to_all.15 = bf16[8,64,128]{2,1,0:T(8,128)(2,1)S(1)} all-to-all(bf16[8,64,128]{2,1,0:T(8,128)(2,1)} %shard_map.97), channel_id=1, replica_groups=mesh['zh'=2,'y'=4,'c'=2,'zl'=4,'x'=4] {'zh','zl'}, dimensions={0} | all-to-all | bytes 262144 | tf_op jit(solution)/shard_map/all_to_all | solution.py:306
  183.0 0.9 shard_map.98
  183.8 6.4 %all-to-all-start.2 = ((bf16[32,2,32,128]{3,2,1,0:T(8,128)(2,1)}), bf16[32,2,32,128]{3,2,1,0:T(8,128)(2,1)S(1)}, u32[]{:S(2)}, u32[]{:S(2)}) async-start(bf16[32,2,32,128]{3,2,1,0:T(8,128)(2,1)} %shard_map.98), calls=%async_computation.2 | async-start | bytes 1048576 | tf_op jit(solution)/shard_map/all_to_all | solution.py:306
  190.2 11.4 %all-to-all-done.2 = bf16[32,2,32,128]{3,2,1,0:T(8,128)(2,1)S(1)} async-done(((bf16[32,2,32,128]{3,2,1,0:T(8,128)(2,1)}), bf16[32,2,32,128]{3,2,1,0:T(8,128)(2,1)S(1)}, u32[]{:S(2)}, u32[]{:S(2)}) %all-to-all-start.2) | async-done | bytes 524320 | tf_op jit(solution)/shard_map/all_to_all | solution.py:306
  201.7 3.2 %shard_map.99 = (f32[1,4096]{1,0:T(1,128)}, f32[16,256]{1,0:T(8,128)}) custom-call(s32[1]{0:T(128)} %bitcast.me_ref, bf16[4,4,2,2,32,128]{5,4,3,2,1,0:T(8,128)(2,1)S(1)} %bitcast.15, bf16[256,4096]{1,0:T(8,128)(2,1)} %q_hbm.1), custom_call_target="tpu_custom_call" | custom-call | tf_op jit(solution)/shard_map/pallas_call | solution.py:276
  (50 shorter events, 3.8 us)
Async XLA Ops:
  0.6 69.2 %copy-start = (bf16[256,512]{1,0:T(8,128)(2,1)S(1)}, bf16[256,512]{1,0:T(8,128)(2,1)}, u32[]{:S(2)}) copy-start(bf16[256,512]{1,0:T(8,128)(2,1)} %param.8) | copy-start | bytes 786436
  0.6 40.7 %collective-permute-start.9 = (bf16[1792,512]{1,0:T(8,128)(2,1)}, bf16[1792,512]{1,0:T(8,128)(2,1)}, u32[]{:S(2)}, u32[]{:S(2)}) collective-permute-start(bf16[1792,512]{1,0:T(8,128)(2,1)} %refs_9_.1), channel_id=1, source_target_pairs={{0,32},{16,112},{32,64},{48,16},{64,96},{80,48},{96,0},{112,80},{1... | collective-permute-start | bytes 5505032 | tf_op jit(solution)/shard_map/ppermute | solution.py:302
  4.3 94.4 %collective-permute-start.11 = (bf16[1792,512]{1,0:T(8,128)(2,1)}, bf16[1792,512]{1,0:T(8,128)(2,1)}, u32[]{:S(2)}, u32[]{:S(2)}) collective-permute-start(bf16[1792,512]{1,0:T(8,128)(2,1)} %refs_9_.1), channel_id=1, source_target_pairs={{0,96},{16,48},{32,0},{48,80},{64,32},{80,112},{96,64},{112,16},{1... | collective-permute-start | bytes 5505032 | tf_op jit(solution)/shard_map/ppermute | solution.py:302
  41.4 57.4 %collective-permute-start.13 = (bf16[1792,512]{1,0:T(8,128)(2,1)}, bf16[1792,512]{1,0:T(8,128)(2,1)}, u32[]{:S(2)}, u32[]{:S(2)}) collective-permute-start(bf16[1792,512]{1,0:T(8,128)(2,1)} %collective-permute-done.9.refs_11_), channel_id=1, source_target_pairs={{0,32},{16,112},{32,64},{48,16},{64,96},{80,48},{96,0},{112,80},{1... | collective-permute-start | bytes 5505032 | tf_op jit(solution)/shard_map/ppermute | solution.py:302
  44.8 57.0 %copy-start.4 = (s32[1792,64]{0,1:T(8,128)S(1)}, s32[1792,64]{0,1:T(8,128)}, u32[]{:S(2)}) copy-start(s32[1792,64]{0,1:T(8,128)} %param.14) | copy-start | bytes 1376260
  45.8 15.9 %collective-permute-start = (bf16[128,1024]{1,0:T(8,128)(2,1)S(1)}, bf16[128,1024]{1,0:T(8,128)(2,1)S(1)}, u32[]{:S(2)}, u32[]{:S(2)}) collective-permute-start(bf16[128,1024]{1,0:T(8,128)(2,1)S(1)} %dynamic_slice.3), channel_id=1, source_target_pairs={{0,128},{128,0},{1,129},{129,1},{2,130},{130,2},{3,131},{131,3},{4... | collective-permute-start | bytes 786440 | tf_op jit(solution)/shard_map/ppermute | solution.py:20
  61.7 40.4 %copy-start.5 = (bf16[128,1024]{1,0:T(8,128)(2,1)}, bf16[128,1024]{1,0:T(8,128)(2,1)S(1)}, u32[]{:S(2)}) copy-start(bf16[128,1024]{1,0:T(8,128)(2,1)S(1)} %collective-permute-done.refs_1_) | copy-start | bytes 786436
  61.7 20.9 %collective-permute-start.1 = (bf16[128,1024]{1,0:T(8,128)(2,1)S(1)}, bf16[128,1024]{1,0:T(8,128)(2,1)S(1)}, u32[]{:S(2)}, u32[]{:S(2)}) collective-permute-start(bf16[128,1024]{1,0:T(8,128)(2,1)S(1)} %collective-permute-done.refs_1_), channel_id=1, source_target_pairs={{1,0},{2,1},{3,2},{0,3},{5,4},{6,5},{7,6},{4,7},{9,8},{10,9},{11,1... | collective-permute-start | bytes 786440 | tf_op jit(solution)/shard_map/ppermute | solution.py:24
  64.5 19.6 %collective-permute-start.4 = (bf16[128,1024]{1,0:T(8,128)(2,1)S(1)}, bf16[128,1024]{1,0:T(8,128)(2,1)S(1)}, u32[]{:S(2)}, u32[]{:S(2)}) collective-permute-start(bf16[128,1024]{1,0:T(8,128)(2,1)S(1)} %collective-permute-done.refs_1_), channel_id=1, source_target_pairs={{0,4},{4,0},{8,12},{12,8},{1,5},{5,1},{9,13},{13,9},{2,6},{6,2},{1... | collective-permute-start | bytes 786440 | tf_op jit(solution)/shard_map/ppermute | solution.py:322
  71.2 4.1 %collective-permute-start.18 = (bf16[64,256]{1,0:T(8,128)(2,1)S(1)}, bf16[64,256]{1,0:T(8,128)(2,1)S(1)}, u32[]{:S(2)}, u32[]{:S(2)}) collective-permute-start(bf16[64,256]{1,0:T(8,128)(2,1)S(1)} %fusion.7), channel_id=1, source_target_pairs={{3,0},{0,1},{1,2},{2,3},{7,4},{4,5},{5,6},{6,7},{11,8},{8,9},{9,10... | collective-permute-start | bytes 98312 | tf_op jit(solution)/shard_map/ppermute | solution.py:24
  75.2 4.3 %collective-permute-start.17 = (bf16[64,256]{1,0:T(8,128)(2,1)S(1)}, bf16[64,256]{1,0:T(8,128)(2,1)S(1)}, u32[]{:S(2)}, u32[]{:S(2)}) collective-permute-start(bf16[64,256]{1,0:T(8,128)(2,1)S(1)} %fusion.7), channel_id=1, source_target_pairs={{2,0},{3,1},{0,2},{1,3},{6,4},{7,5},{4,6},{5,7},{10,8},{11,9},{8,1... | collective-permute-start | bytes 98312 | tf_op jit(solution)/shard_map/ppermute | solution.py:24
  79.5 3.1 %collective-permute-start.16 = (bf16[64,256]{1,0:T(8,128)(2,1)S(1)}, bf16[64,256]{1,0:T(8,128)(2,1)S(1)}, u32[]{:S(2)}, u32[]{:S(2)}) collective-permute-start(bf16[64,256]{1,0:T(8,128)(2,1)S(1)} %fusion.7), channel_id=1, source_target_pairs={{1,0},{2,1},{3,2},{0,3},{5,4},{6,5},{7,6},{4,7},{9,8},{10,9},{11,1... | collective-permute-start | bytes 98312 | tf_op jit(solution)/shard_map/ppermute | solution.py:24
  82.6 6.8 %collective-permute-start.2 = (bf16[128,1024]{1,0:T(8,128)(2,1)S(1)}, bf16[128,1024]{1,0:T(8,128)(2,1)S(1)}, u32[]{:S(2)}, u32[]{:S(2)}) collective-permute-start(bf16[128,1024]{1,0:T(8,128)(2,1)S(1)} %collective-permute-done.refs_1_), channel_id=1, source_target_pairs={{2,0},{3,1},{0,2},{1,3},{6,4},{7,5},{4,6},{5,7},{10,8},{11,9},{8,1... | collective-permute-start | bytes 786440 | tf_op jit(solution)/shard_map/ppermute | solution.py:24
  82.6 19.5 %copy-start.6 = (bf16[128,1024]{1,0:T(8,128)(2,1)}, bf16[128,1024]{1,0:T(8,128)(2,1)S(1)}, u32[]{:S(2)}) copy-start(bf16[128,1024]{1,0:T(8,128)(2,1)S(1)} %collective-permute-done.1.refs_2_) | copy-start | bytes 786436
  82.6 13.2 %collective-permute-start.3 = (bf16[128,1024]{1,0:T(8,128)(2,1)S(1)}, bf16[128,1024]{1,0:T(8,128)(2,1)S(1)}, u32[]{:S(2)}, u32[]{:S(2)}) collective-permute-start(bf16[128,1024]{1,0:T(8,128)(2,1)S(1)} %collective-permute-done.refs_1_), channel_id=1, source_target_pairs={{3,0},{0,1},{1,2},{2,3},{7,4},{4,5},{5,6},{6,7},{11,8},{8,9},{9,10... | collective-permute-start | bytes 786440 | tf_op jit(solution)/shard_map/ppermute | solution.py:24
  84.1 18.8 %copy-start.7 = (bf16[128,1024]{1,0:T(8,128)(2,1)}, bf16[128,1024]{1,0:T(8,128)(2,1)S(1)}, u32[]{:S(2)}) copy-start(bf16[128,1024]{1,0:T(8,128)(2,1)S(1)} %collective-permute-done.4.refs_5_) | copy-start | bytes 786436
  84.1 11.7 %collective-permute-start.5 = (bf16[128,1024]{1,0:T(8,128)(2,1)S(1)}, bf16[128,1024]{1,0:T(8,128)(2,1)S(1)}, u32[]{:S(2)}, u32[]{:S(2)}) collective-permute-start(bf16[128,1024]{1,0:T(8,128)(2,1)S(1)} %collective-permute-done.4.refs_5_), channel_id=1, source_target_pairs={{1,0},{2,1},{3,2},{0,3},{5,4},{6,5},{7,6},{4,7},{9,8},{10,9},{11,1... | collective-permute-start | bytes 786440 | tf_op jit(solution)/shard_map/ppermute | solution.py:24
  89.4 9.4 %copy-start.8 = (bf16[128,1024]{1,0:T(8,128)(2,1)}, bf16[128,1024]{1,0:T(8,128)(2,1)S(1)}, u32[]{:S(2)}) copy-start(bf16[128,1024]{1,0:T(8,128)(2,1)S(1)} %collective-permute-done.2.refs_3_) | copy-start | bytes 786436
  89.4 31.2 %collective-permute-start.8 = (bf16[1792,512]{1,0:T(8,128)(2,1)}, bf16[1792,512]{1,0:T(8,128)(2,1)}, u32[]{:S(2)}, u32[]{:S(2)}) collective-permute-start(bf16[1792,512]{1,0:T(8,128)(2,1)} %refs_9_.1), channel_id=1, source_target_pairs={{0,16},{16,0},{1,17},{17,1},{2,18},{18,2},{3,19},{19,3},{4,20},{20... | collective-permute-start | bytes 5505032 | tf_op jit(solution)/shard_map/ppermute | solution.py:20
  95.7 3.1 %copy-start.9 = (bf16[128,1024]{1,0:T(8,128)(2,1)}, bf16[128,1024]{1,0:T(8,128)(2,1)S(1)}, u32[]{:S(2)}) copy-start(bf16[128,1024]{1,0:T(8,128)(2,1)S(1)} %collective-permute-done.3.refs_4_) | copy-start | bytes 786436
  95.7 7.1 %collective-permute-start.6 = (bf16[128,1024]{1,0:T(8,128)(2,1)S(1)}, bf16[128,1024]{1,0:T(8,128)(2,1)}, u32[]{:S(2)}, u32[]{:S(2)}) collective-permute-start(bf16[128,1024]{1,0:T(8,128)(2,1)S(1)} %collective-permute-done.4.refs_5_), channel_id=1, source_target_pairs={{2,0},{3,1},{0,2},{1,3},{6,4},{7,5},{4,6},{5,7},{10,8},{11,9},{8,1... | collective-permute-start | bytes 786440 | tf_op jit(solution)/shard_map/ppermute | solution.py:24
  95.8 3.0 %copy-start.10 = (bf16[128,1024]{1,0:T(8,128)(2,1)}, bf16[128,1024]{1,0:T(8,128)(2,1)S(1)}, u32[]{:S(2)}) copy-start(bf16[128,1024]{1,0:T(8,128)(2,1)S(1)} %collective-permute-done.5.refs_6_) | copy-start | bytes 786436
  95.8 24.9 %collective-permute-start.10 = (bf16[1792,512]{1,0:T(8,128)(2,1)}, bf16[1792,512]{1,0:T(8,128)(2,1)}, u32[]{:S(2)}, u32[]{:S(2)}) collective-permute-start(bf16[1792,512]{1,0:T(8,128)(2,1)} %collective-permute-done.9.refs_11_), channel_id=1, source_target_pairs={{0,16},{16,0},{1,17},{17,1},{2,18},{18,2},{3,19},{19,3},{4,20},{20... | collective-permute-start | bytes 5505032 | tf_op jit(solution)/shard_map/ppermute | solution.py:20
  98.7 21.9 %collective-permute-start.12 = (bf16[1792,512]{1,0:T(8,128)(2,1)}, bf16[1792,512]{1,0:T(8,128)(2,1)}, u32[]{:S(2)}, u32[]{:S(2)}) collective-permute-start(bf16[1792,512]{1,0:T(8,128)(2,1)} %collective-permute-done.11.refs_13_), channel_id=1, source_target_pairs={{0,16},{16,0},{1,17},{17,1},{2,18},{18,2},{3,19},{19,3},{4,20},{20... | collective-permute-start | bytes 5505032 | tf_op jit(solution)/shard_map/ppermute | solution.py:20
  98.8 62.3 %collective-permute-start.14 = (bf16[1792,512]{1,0:T(8,128)(2,1)}, bf16[1792,512]{1,0:T(8,128)(2,1)}, u32[]{:S(2)}, u32[]{:S(2)}) collective-permute-start(bf16[1792,512]{1,0:T(8,128)(2,1)} %collective-permute-done.13.mat_ref), channel_id=1, source_target_pairs={{0,16},{16,0},{1,17},{17,1},{2,18},{18,2},{3,19},{19,3},{4,20},{20... | collective-permute-start | bytes 5505032 | tf_op jit(solution)/shard_map/ppermute | solution.py:20
  101.7 13.7 %copy-start.1 = (bf16[256,1792]{1,0:T(8,128)(2,1)}, bf16[256,1792]{1,0:T(8,128)(2,1)S(1)}, u32[]{:S(2)}) copy-start(bf16[256,1792]{1,0:T(8,128)(2,1)S(1)} %fusion.5.refs_15_.act_ref.near_hbm) | copy-start | bytes 2752516
  102.8 6.4 %collective-permute-start.7 = (bf16[128,1024]{1,0:T(8,128)(2,1)S(1)}, bf16[128,1024]{1,0:T(8,128)(2,1)S(1)}, u32[]{:S(2)}, u32[]{:S(2)}) collective-permute-start(bf16[128,1024]{1,0:T(8,128)(2,1)S(1)} %collective-permute-done.4.refs_5_), channel_id=1, source_target_pairs={{3,0},{0,1},{1,2},{2,3},{7,4},{4,5},{5,6},{6,7},{11,8},{8,9},{9,10... | collective-permute-start | bytes 786440 | tf_op jit(solution)/shard_map/ppermute | solution.py:24
  109.3 11.4 %copy-start.11 = (bf16[128,1024]{1,0:T(8,128)(2,1)}, bf16[128,1024]{1,0:T(8,128)(2,1)S(1)}, u32[]{:S(2)}) copy-start(bf16[128,1024]{1,0:T(8,128)(2,1)S(1)} %collective-permute-done.7.refs_8_) | copy-start | bytes 786436
  109.3 51.9 %collective-permute-start.15 = (bf16[256,1792]{1,0:T(8,128)(2,1)S(1)}, bf16[256,1792]{1,0:T(8,128)(2,1)S(1)}, u32[]{:S(2)}, u32[]{:S(2)}) collective-permute-start(bf16[256,1792]{1,0:T(8,128)(2,1)S(1)} %fusion.5.refs_15_.act_ref.near_hbm), channel_id=1, source_target_pairs={{0,128},{128,0},{1,129},{129,1},{2,130},{130,2},{3,131},{131,3},{4... | collective-permute-start | bytes 2752520 | tf_op jit(solution)/shard_map/ppermute | solution.py:20
  115.4 45.7 %all-to-all-start = ((bf16[8,64,256]{2,1,0:T(8,128)(2,1)}), bf16[8,64,256]{2,1,0:T(8,128)(2,1)S(1)}, u32[]{:S(2)}, u32[]{:S(2)}) async-start(bf16[8,64,256]{2,1,0:T(8,128)(2,1)} %broadcast_in_dim.2), calls=%async_computation | async-start | bytes 524288 | tf_op jit(solution)/shard_map/all_to_all | solution.py:29
  161.2 1.1 copy-start.3
  183.8 17.8 %all-to-all-start.2 = ((bf16[32,2,32,128]{3,2,1,0:T(8,128)(2,1)}), bf16[32,2,32,128]{3,2,1,0:T(8,128)(2,1)S(1)}, u32[]{:S(2)}, u32[]{:S(2)}) async-start(bf16[32,2,32,128]{3,2,1,0:T(8,128)(2,1)} %shard_map.98), calls=%async_computation.2 | async-start | bytes 1048576 | tf_op jit(solution)/shard_map/all_to_all | solution.py:306
  (1 other events, 0.7 us)
